TPU v7x, 32 devices: a whole 2x2x4 slice. The times are simulated.
32 devices in a mesh: row: 8 (over z, y), col: 4 (over x, core).
Axes of the slice: x: 2, y: 2, z: 4, core: 2. Of those that a mesh axis runs over, the one named last changes fastest.
Arguments:
- saved_inputs: bfloat16 [8192, 4096], P(('row', 'col')), may hold values from -6 to 6
- output_grads: bfloat16 [8192, 14336], P(('row', 'col')), may hold values from -0.5 to 0.5
- proj_in: bfloat16 [4096, 128], replicated, may hold values from -0.09375 to 0.09375
- proj_out: bfloat16 [14336, 128], replicated, may hold values from -0.046875 to 0.046875
- doc_lengths: int32 [32], replicated, may hold values from 64 to 448, as said below
- device_docs: int32 [32], replicated, may hold values from 0 to 31, as said below
- fisher_inverse: float32 [16384, 16384], P('row', 'col'), may hold values from -0.3 to 2.3, as said below
Outputs:
- preconditioned: float32 [32, 16384], P('row', 'col')
Inputs may be any that keep to these rules, and one draw needn't show every extreme that they name: `doc_lengths`: the lengths sum to 8192; some document has exactly 448 tokens and some exactly 64. `device_docs`: A permutation of the documents. `fisher_inverse`: Symmetric.
All inputs are finite; a program needn't handle non-finite values.
Results may differ from a plain program's by a relative error of at most 0.0041.
Values sent between devices are 32-bit elements; how exact they have to be, the bound alone decides.
No kernel may reach another device: no remote copies, remote signals or barrier semaphores. Data moves between devices by JAX's collectives and lax.ppermute only.
A program may use at most 128 MiB of HBM per device.

v0:
```python
import jax
import jax.numpy as jnp
from jax import lax
from jax.sharding import PartitionSpec as P

SLOTS = 5


def per_device(
    saved_inputs, output_grads, proj_in, proj_out, doc_lengths, device_docs, fisher_inverse
):
    tok_count = saved_inputs.shape[0]
    n_row = lax.axis_size("row")
    n_col = lax.axis_size("col")
    devices = n_row * n_col
    rank_in = proj_in.shape[1]
    rank_out = proj_out.shape[1]
    feat_count = rank_in * rank_out
    shard_index = lax.axis_index("row") * n_col + lax.axis_index("col")
    low_in = jnp.dot(saved_inputs, proj_in, preferred_element_type=jnp.float32).astype(jnp.bfloat16)
    low_out = jnp.dot(output_grads, proj_out, preferred_element_type=jnp.float32).astype(
        jnp.bfloat16
    )
    doc_ends = jnp.cumsum(doc_lengths)
    starts = doc_ends - doc_lengths
    positions = shard_index * tok_count + jnp.arange(tok_count, dtype=jnp.int32)
    doc_ids = jnp.sum((starts[None, :] <= positions[:, None]).astype(jnp.int32), axis=1) - 1
    first_doc = doc_ids[0]
    slot_range = jnp.arange(SLOTS, dtype=jnp.int32)
    slot_masks = (doc_ids[:, None] - first_doc == slot_range[None, :]).astype(jnp.bfloat16)
    masked = (slot_masks[:, :, None] * low_out[:, None, :]).reshape(tok_count, SLOTS * rank_out)
    partials = lax.dot_general(
        masked, low_in, (((0,), (0,)), ((), ())), preferred_element_type=jnp.float32
    )
    partials = partials.reshape(SLOTS, feat_count)
    exchanged = lax.all_to_all(partials, "row", split_axis=1, concat_axis=0, tiled=True)
    gathered = lax.all_gather(exchanged, "col", axis=0, tiled=True)
    device_starts = jnp.arange(devices, dtype=jnp.int32) * tok_count
    firsts_all = jnp.sum((starts[None, :] <= device_starts[:, None]).astype(jnp.int32), axis=1) - 1
    slot_docs = firsts_all.reshape(n_row, n_col).T[:, :, None] + slot_range[None, None, :]
    onehot = (device_docs[:, None] == slot_docs.reshape(1, -1)).astype(jnp.float32)
    doc_block = jnp.dot(
        onehot, gathered, precision=lax.Precision.HIGHEST, preferred_element_type=jnp.float32
    )
    return lax.psum_scatter(
        jnp.dot(
            doc_block,
            fisher_inverse,
            precision=lax.Precision.HIGHEST,
            preferred_element_type=jnp.float32,
        ),
        "row",
        scatter_dimension=0,
        tiled=True,
    )


def solution(mesh):
    placed = (P(("row", "col"), None), P(("row", "col"), None), P(), P(), P(), P(), P("row", "col"))
    return jax.shard_map(
        per_device, mesh=mesh, in_specs=placed, out_specs=P("row", "col"), check_vma=False
    )
```

profile of v0, /device:TPU:0, one launch (start us, length us, event | category | flops | bytes accessed | tf_op | source)
XLA Modules:
  0.0 164.9 jit_solution(17696912829641081840)
XLA Ops:
  6.5 0.9 copy.18
  7.5 0.1 reduce
  7.6 0.7 sub.24
  8.3 0.1 convert_reduce_fusion
  8.4 0.5 slice.3
  8.9 0.6 broadcast_subtract_fusion
  9.5 6.2 %convolution_convert_fusion.1 = bf16[256,128]{1,0:T(8,128)(2,1)S(1)} fusion(bf16[256,14336]{1,0:T(8,128)(2,1)} %param.8, bf16[14336,128]{1,0:T(8,128)(2,1)} %param.10), kind=kOutput, calls=%fused_computation.1 | convolution fusion | flops 939556864 | bytes 11075584 | tf_op jit(solution)/shard_map/dot_general | solution.py:21
  15.7 0.1 copy.20
  15.9 2.1 %fusion = f32[640,128]{1,0:T(8,128)S(1)} fusion(bf16[256,640]{0,1:T(8,128)(2,1)S(1)} %bitcast.15, bf16[256,4096]{1,0:T(8,128)(2,1)S(1)} %copy-done, bf16[4096,128]{1,0:T(8,128)(2,1)} %param.9), kind=kOutput, calls=%fused_computation.2 | convolution fusion | flops 310411264 | bytes 3801088 | tf_op jit(solution)/shard_map/dot_general | solution.py:32
  18.0 0.1 all_to_all.14
  18.1 0.2 copy.21
  18.3 21.6 %all_to_all.19 = f32[5,8,2048]{2,0,1:T(8,128)S(1)} all-to-all(f32[5,8,2048]{2,0,1:T(8,128)S(1)} %copy.21), channel_id=1, replica_groups=mesh['row'=8,'col'=4] {'row'}, dimensions={1} | all-to-all | bytes 655360 | tf_op jit(solution)/shard_map/all_to_all | solution.py:36
  40.0 0.8 all_to_all.17
  40.8 0.2 convert_reduce_fusion.1
  41.0 0.1 sub.26
  41.1 0.1 copy.19
  41.2 0.1 iota_add_fusion
  41.3 0.1 add.46
  41.4 16.7 %all-gather.2.cloned.1.call-done = f32[160,2048]{1,0:T(8,128)} async-done(((f32[40,2048]{1,0:T(8,128)}), f32[160,2048]{1,0:T(8,128)}) %all-gather.2.cloned.1.call-update) | async-done | bytes 1310736 | tf_op jit(solution)/shard_map/all_gather | solution.py:37
  58.1 1.9 %fusion.1 = f32[32,2048]{1,0:T(8,128)S(1)} fusion(f32[160,2048]{1,0:T(8,128)} %all-gather.2.cloned.1.call-done, s32[160]{0:T(256)S(1)} %add.46, s32[32]{0:T(128)S(1)} %copy-done.1), kind=kOutput, calls=%fused_computation.5 | convolution fusion | flops 125834240 | bytes 1573632 | tf_op jit(solution)/shard_map/dot_general | solution.py:42
  60.0 23.6 %fusion.6 = f32[32,4096]{1,0:T(8,128)} fusion(f32[32,2048]{1,0:T(8,128)S(1)} %fusion.1, f32[2048,4096]{1,0:T(8,128)} %param.13), kind=kOutput, calls=%fused_computation.19 | convolution fusion | flops 3221225472 | bytes 34340864 | tf_op jit(solution)/shard_map/dot_general | solution.py:46
  83.7 0.6 dynamic-slice
  84.9 71.6 %all-reduce.3.cloned.1.call-done = f32[32,4096]{1,0:T(8,128)} async-done(((f32[32,4096]{1,0:T(8,128)}), f32[32,4096]{1,0:T(8,128)}) %all-reduce.3.cloned.1.call-update) | async-done | bytes 524304
  156.5 1.5 constant_dynamic-slice_fusion
  (17 shorter events, 0.2 us)
Async XLA Ops:
  6.5 9.4 %copy-start = (bf16[256,4096]{1,0:T(8,128)(2,1)S(1)}, bf16[256,4096]{1,0:T(8,128)(2,1)}, u32[]{:S(2)}) copy-start(bf16[256,4096]{1,0:T(8,128)(2,1)} %param.7) | copy-start | bytes 6291460
  6.5 51.6 %all-gather.2.cloned.1.call-start = ((), (), s32[]{:S(2)}) async-start(), calls=%async_computation.1 | async-start | bytes 1638400 | tf_op jit(solution)/shard_map/all_gather | solution.py:37
  15.9 42.2 %copy-start.1 = (s32[32]{0:T(128)S(1)}, s32[32]{0:T(128)}, u32[]{:S(2)}) copy-start(s32[32]{0:T(128)} %param.12) | copy-start | bytes 388
  40.8 115.7 %all-reduce.3.cloned.1.call-start = ((), (), s32[]{:S(2)}) async-start(), calls=%async_computation.2 | async-start | bytes 1048576
  60.0 23.7 %copy-start.2 = (u32[32]{0:T(128)S(1)}, u32[32]{0:T(128)}, u32[]{:S(2)}) copy-start(u32[32]{0:T(128)} %constant.26) | copy-start | bytes 388
Sparse Core Ops, SparseCore 0:
  40.9 17.1 all-gather.1
  83.8 72.6 all-reduce.2
where the time goes:
time: 165 us
  waiting for transfers between devices  88.3 us (54%)
  matrix products  33.8 us (20%)
  blocking collectives  21.6 us (13%)
  between operations  14.2 us (9%)
  local copies, waits for them, and re-layouts  5 us (3%)
  other arithmetic  1.88 us (1%)
    unnamed x3, waiting for transfers between devices  71.6 us
    dot_general x1, matrix products, per_device(): jnp.dot(doc_block, fisher_inverse, precision=lax.Precision.HIGHEST, prefe...  23.6 us
    all_to_all x1, blocking collectives, per_device(): lax.all_to_all(partials, 'row', split_axis=1, concat_axis=0, tiled=True)  21.6 us
    all_gather x1, waiting for transfers between devices, per_device(): gathered = lax.all_gather(exchanged, 'col', axis=0, tiled=True)  16.7 us
    dot_general x1, matrix products, per_device(): jnp.dot(output_grads, proj_out, preferred_element_type=jnp.float32)  6.19 us
  transfers between devices with their start and end apart: 2, of which 2 were waited for; matrix products, arithmetic and copies ran while one was open for 1% of the time, Pallas kernels for 0%

commit v1 on v0

v1 whole, which is shorter than its diff:
```python
import functools

import jax
import jax.numpy as jnp
from jax import lax
from jax.experimental import pallas as pl
from jax.experimental.pallas import tpu as pltpu
from jax.sharding import PartitionSpec as P

SLOTS = 5
STEPS = 8
MIB = 1024 * 1024


def doc_ends(lens):
    docs = lens.shape[1]
    row = lax.broadcasted_iota(jnp.int32, (docs, docs), 0)
    col = lax.broadcasted_iota(jnp.int32, (docs, docs), 1)
    wide = jnp.broadcast_to(lens.astype(jnp.float32), (docs, docs))
    return jnp.sum(jnp.where(col <= row, wide, 0.0), axis=1, keepdims=True)


def docs_at(ends, positions):
    return jnp.sum(jnp.where(ends <= positions, 1.0, 0.0), axis=0, keepdims=True)


def partials_kernel(n_col, lens, x_in, x_out, w_in, w_out, out, acc_in, acc_out):
    step = pl.program_id(0)

    @pl.when(step == 0)
    def _():
        acc_in[...] = jnp.zeros_like(acc_in)
        acc_out[...] = jnp.zeros_like(acc_out)

    acc_in[...] += jnp.dot(x_in[...], w_in[...], preferred_element_type=jnp.float32)
    acc_out[...] += jnp.dot(x_out[...], w_out[...], preferred_element_type=jnp.float32)

    @pl.when(step == pl.num_programs(0) - 1)
    def _():
        tokens = acc_out.shape[0]
        shard = lax.axis_index("row") * n_col + lax.axis_index("col")
        base = (shard * tokens).astype(jnp.float32)
        ends = doc_ends(lens[...])
        token = lax.broadcasted_iota(jnp.int32, (1, tokens), 1).astype(jnp.float32)
        slot = docs_at(ends, token + base) - docs_at(ends, jnp.zeros((1, tokens)) + base)
        low_in = acc_in[...].astype(jnp.bfloat16)
        low_out = acc_out[...].astype(jnp.bfloat16).astype(jnp.float32).T
        devices, _, rows, _ = out.shape
        for s in range(SLOTS):
            masked = jnp.where(slot == float(s), low_out, 0.0).astype(jnp.bfloat16)
            part = jnp.dot(masked, low_in, preferred_element_type=jnp.float32)
            for j in range(devices):
                out[j, s] = part[j * rows : (j + 1) * rows]


def partials_call(x_in, x_out, w_in, w_out, lens, n_col, devices):
    tokens, d_in = x_in.shape
    d_out, rank_out = w_out.shape
    rank_in = w_in.shape[1]
    k_in, k_out = d_in // STEPS, d_out // STEPS
    return pl.pallas_call(
        functools.partial(partials_kernel, n_col),
        grid=(STEPS,),
        in_specs=[
            pl.BlockSpec(lens.shape, lambda i: (0, 0)),
            pl.BlockSpec((tokens, k_in), lambda i: (0, i)),
            pl.BlockSpec((tokens, k_out), lambda i: (0, i)),
            pl.BlockSpec((k_in, rank_in), lambda i: (i, 0)),
            pl.BlockSpec((k_out, rank_out), lambda i: (i, 0)),
        ],
        out_specs=pl.BlockSpec(
            (devices, SLOTS, rank_out // devices, rank_in), lambda i: (0, 0, 0, 0)
        ),
        out_shape=jax.ShapeDtypeStruct(
            (devices, SLOTS, rank_out // devices, rank_in), jnp.float32
        ),
        scratch_shapes=[
            pltpu.VMEM((tokens, rank_in), jnp.float32),
            pltpu.VMEM((tokens, rank_out), jnp.float32),
        ],
        compiler_params=pltpu.CompilerParams(vmem_limit_bytes=16 * MIB),
        name="partials",
    )(lens, x_in, x_out, w_in, w_out)


def narrow_kernel(f_ref, out):
    out[...] = f_ref[...].astype(jnp.bfloat16)


def narrow_call(fisher):
    rows, cols = fisher.shape
    step = min(rows, 128)
    return pl.pallas_call(
        narrow_kernel,
        grid=(rows // step,),
        in_specs=[pl.BlockSpec((step, cols), lambda i: (i, 0))],
        out_specs=pl.BlockSpec((step, cols), lambda i: (i, 0)),
        out_shape=jax.ShapeDtypeStruct((rows, cols), jnp.bfloat16),
        compiler_params=pltpu.CompilerParams(vmem_limit_bytes=16 * MIB),
        cost_estimate=pl.CostEstimate(
            flops=rows * cols, bytes_accessed=6 * rows * cols, transcendentals=0
        ),
        name="narrow",
    )(fisher)


def combine_kernel(tokens, lens, docs_row, got, out):
    docs = lens.shape[1]
    pieces, rank = got.shape
    rows = out.shape[1] // rank
    slots = pieces // rows
    ends = doc_ends(lens[...])
    m = lax.broadcasted_iota(jnp.int32, (1, slots), 1)
    source = lax.shift_right_logical(m * 52429, 18)
    first = docs_at(ends, (source * tokens).astype(jnp.float32))
    doc = first + (m - source * SLOTS).astype(jnp.float32)
    row = lax.broadcasted_iota(jnp.int32, (docs, docs), 0)
    col = lax.broadcasted_iota(jnp.int32, (docs, docs), 1)
    wanted = jnp.broadcast_to(docs_row[...].astype(jnp.float32), (docs, docs))
    wanted = jnp.sum(jnp.where(col == row, wanted, 0.0), axis=1, keepdims=True)
    onehot = jnp.where(wanted == doc, 1.0, 0.0)
    for p in range(rows):
        piece = got[pl.ds(p, slots, stride=rows), :]
        out[:, p * rank : (p + 1) * rank] = jnp.dot(
            onehot, piece, precision=lax.Precision.HIGHEST, preferred_element_type=jnp.float32
        )


def combine_call(got, lens, docs_row, tokens):
    devices, slots, rows, rank = got.shape
    docs = lens.shape[1]
    return pl.pallas_call(
        functools.partial(combine_kernel, tokens),
        out_shape=jax.ShapeDtypeStruct((docs, rows * rank), jnp.float32),
        compiler_params=pltpu.CompilerParams(vmem_limit_bytes=16 * MIB),
        name="combine",
    )(lens, docs_row, got.reshape(devices * slots * rows, rank))


def product_kernel(n_parts, *refs):
    parts, (f_ref, out) = refs[:n_parts], refs[n_parts:]
    docs, size = parts[0].shape
    me = lax.axis_index("col")
    groups, rows, _ = out.shape
    highs, lows = [], []
    for part in parts:
        high = part[...].astype(jnp.bfloat16)
        highs.append(high)
        lows.append((part[...] - high.astype(jnp.float32)).astype(jnp.bfloat16))
    both = [jnp.concatenate([h, l], axis=0) for h, l in zip(highs, lows)]
    cols = f_ref.shape[1]
    width = 512 if cols % 512 == 0 else cols
    for n in range(cols // width):
        total = jnp.zeros((2 * docs, width), jnp.float32)
        for k in range(n_parts):
            at = pl.multiple_of(jnp.bitwise_xor(me, k) * size, size)
            tile = f_ref[pl.ds(at, size), n * width : (n + 1) * width]
            total += jnp.dot(both[k], tile, preferred_element_type=jnp.float32)
        total = total[:docs] + total[docs:]
        for g in range(groups):
            out[g, :, n * width : (n + 1) * width] = total[g * rows : (g + 1) * rows]


def product_call(parts, fisher, groups):
    docs = parts[0].shape[0]
    cols = fisher.shape[1]
    n = len(parts)
    return pl.pallas_call(
        functools.partial(product_kernel, n),
        out_shape=jax.ShapeDtypeStruct((groups, docs // groups, cols), jnp.float32),
        compiler_params=pltpu.CompilerParams(vmem_limit_bytes=40 * MIB),
        name="product",
    )(*parts, fisher)


def exchange(x, axis, bit):
    size = lax.axis_size(axis)
    return lax.ppermute(x, axis, [(i, i ^ bit) for i in range(size)])


def per_device(
    saved_inputs, output_grads, proj_in, proj_out, doc_lengths, device_docs, fisher_inverse
):
    tokens = saved_inputs.shape[0]
    n_row, n_col = lax.axis_size("row"), lax.axis_size("col")
    devices = n_row * n_col
    lens = doc_lengths.reshape(1, -1)
    docs_row = device_docs.reshape(1, -1)
    partials = partials_call(
        saved_inputs, output_grads, proj_in, proj_out, lens, n_col, devices
    )
    got = lax.all_to_all(partials, ("row", "col"), 0, 0, tiled=True)
    fisher = narrow_call(fisher_inverse)
    mine = combine_call(got, lens, docs_row, tokens)
    parts = {0: mine}
    bit = n_col // 2
    while bit:
        parts.update({k ^ bit: exchange(v, "col", bit) for k, v in list(parts.items())})
        bit //= 2
    sums = product_call([parts[k] for k in range(n_col)], fisher, n_row)
    shares = lax.all_to_all(sums, "row", 0, 0, tiled=True)
    return jnp.sum(shares, axis=0)


def solution(mesh):
    placed = (P(("row", "col"), None), P(("row", "col"), None), P(), P(), P(), P(), P("row", "col"))
    return jax.shard_map(
        per_device, mesh=mesh, in_specs=placed, out_specs=P("row", "col"), check_vma=False
    )
```

time: 165 us -> 86 us (0.52)
  waiting for transfers between devices: 88.3 us -> 3.84 us
  matrix products: 33.8 us -> 0 us
  Pallas kernels: 0 us -> 29.2 us
  blocking collectives: 21.6 us -> 37 us
  between operations: 14.2 us -> 0.04 us
  local copies, waits for them, and re-layouts: 5 us -> 14.3 us
    unnamed x3 -> x0, waiting for transfers between devices: 71.6 us -> none
    dot_general x4 -> x0, matrix products: 33.8 us -> none  [the longest x1 23.6 us: per_device(): jnp.dot(doc_block, fisher_inverse, precision=lax.Precision.HIGHEST, prefe...]
    pallas_call x0 -> x4, Pallas kernels: none -> 29.2 us  [the longest x1 15.1 us: narrow_call(): pl.pallas_call(narrow_kernel, grid=(rows // step,), in_specs=[pl.BlockSpe...]
    all_gather x1 -> x0, waiting for transfers between devices: 16.7 us -> none  [per_device(): gathered = lax.all_gather(exchanged, 'col', axis=0, tiled=True)]
    all_to_all x1 -> x2, blocking collectives: 21.6 us -> 37 us  [the longest x1 19.2 us: per_device(): got = lax.all_to_all(partials, ('row', 'col'), 0, 0, tiled=True)]
    unnamed x8 -> x14, local copies, waits for them, and re-layouts: 2.15 us -> 14.3 us
    ppermute x0 -> x3, waiting for transfers between devices: none -> 3.84 us  [exchange(): return lax.ppermute(x, axis, [(i, i ^ bit) for i in range(size)])]
  transfers between devices with their start and end apart: 2 -> 3, of which waited for: 2 -> 1; matrix products, arithmetic and copies ran while one was open for 1% -> 0% of each run, Pallas kernels for 0% -> 18%
where the time goes in v1:
time: 86 us; the launch traced here: 85.6 us
  blocking collectives  37 us (43%)
  Pallas kernels  29.2 us (34%)
  local copies, waits for them, and re-layouts  14.3 us (17%)
  waiting for transfers between devices  3.84 us (4%)
    all_to_all x1, blocking collectives, per_device(): got = lax.all_to_all(partials, ('row', 'col'), 0, 0, tiled=True)  19.2 us
    all_to_all x1, blocking collectives, per_device(): shares = lax.all_to_all(sums, 'row', 0, 0, tiled=True)  17.9 us
    pallas_call x1, Pallas kernels, narrow_call(): pl.pallas_call(narrow_kernel, grid=(rows // step,), in_specs=[pl.BlockSpe...  15.1 us
    unnamed x14, local copies, waits for them, and re-layouts  14.3 us
    pallas_call x1, Pallas kernels, product_call(): pl.pallas_call(functools.partial(product_kernel, n), out_shape=jax.ShapeD...  8.78 us
    pallas_call x1, Pallas kernels, partials_call(): pl.pallas_call(functools.partial(partials_kernel, n_col), grid=(STEPS,),...  4.85 us
    ppermute x3, waiting for transfers between devices, exchange(): return lax.ppermute(x, axis, [(i, i ^ bit) for i in range(size)])  3.84 us
  transfers between devices with their start and end apart: 3, of which 1 were waited for; matrix products, arithmetic and copies ran while one was open for 0% of the time, Pallas kernels for 18%

profile of v1, /device:TPU:0, one launch (start us, length us, event | category | flops | bytes accessed | tf_op | source)
XLA Modules:
  0.0 85.6 jit_solution(12864787215791468000)
XLA Ops:
  0.0 0.0 copy-start.1
  0.0 3.1 %copy-done.1 = bf16[256,14336]{1,0:T(8,128)(2,1)S(1)} copy-done((bf16[256,14336]{1,0:T(8,128)(2,1)S(1)}, bf16[256,14336]{1,0:T(8,128)(2,1)}, u32[]{:S(2)}) %copy-start.1) | copy-done | bytes 7340056
  3.1 0.0 copy-start.2
  3.1 2.0 %copy-done.2 = bf16[14336,128]{1,0:T(8,128)(2,1)S(1)} copy-done((bf16[14336,128]{1,0:T(8,128)(2,1)S(1)}, bf16[14336,128]{1,0:T(8,128)(2,1)}, u32[]{:S(2)}) %copy-start.2) | copy-done | bytes 3670040
  5.1 0.0 copy-start.3
  5.1 1.6 %copy-done.3 = bf16[256,4096]{1,0:T(8,128)(2,1)S(1)} copy-done((bf16[256,4096]{1,0:T(8,128)(2,1)S(1)}, bf16[256,4096]{1,0:T(8,128)(2,1)}, u32[]{:S(2)}) %copy-start.3) | copy-done | bytes 2097176
  6.7 1.2 %copy-done.4 = bf16[4096,128]{1,0:T(8,128)(2,1)S(1)} copy-done((bf16[4096,128]{1,0:T(8,128)(2,1)S(1)}, bf16[4096,128]{1,0:T(8,128)(2,1)}, u32[]{:S(2)}) %copy-start.4) | copy-done | bytes 1048600
  7.9 0.7 copy-done.5
  8.6 4.8 %partials.1 = f32[32,5,4,128]{3,2,1,0:T(4,128)S(1)} custom-call(s32[1,32]{1,0:T(1,128)S(1)} %bitcast.4, bf16[256,4096]{1,0:T(8,128)(2,1)S(1)} %copy-done.3, bf16[256,14336]{1,0:T(8,128)(2,1)S(1)} %copy-done.1, bf16[4096,128]{1,0:T(8,128)(2,1)S(1)} %copy-done.4, bf16[14336,128]{1,0:T(8,128)(2,1)S(1)} %copy-done.2), custom_call_target="tpu_custom_call" | custom-call | tf_op jit(solution)/shard_map/partials/pallas_call | solution.py:61
  13.5 19.2 %all_to_all.10 = f32[32,5,4,128]{3,2,1,0:T(4,128)S(1)} all-to-all(f32[32,5,4,128]{3,2,1,0:T(4,128)S(1)} %partials.1), channel_id=1, replica_groups=mesh['row'=8,'col'=4] {'row','col'}, dimensions={0} | all-to-all | bytes 655360 | tf_op jit(solution)/shard_map/all_to_all | solution.py:192
  32.6 0.0 copy-done.6
  32.6 0.5 combine.1.refs_0_
  33.1 0.2 collective-permute-start.1
  33.3 0.3 collective-permute-start
  33.5 3.8 %collective-permute-done.1.refs_2_ = f32[32,512]{1,0:T(8,128)S(1)} collective-permute-done((f32[32,512]{1,0:T(8,128)S(1)}, f32[32,512]{1,0:T(8,128)S(1)}, u32[]{:S(2)}, u32[]{:S(2)}) %collective-permute-start.1) | collective-permute-done | bytes 65568 | tf_op jit(solution)/shard_map/ppermute | solution.py:178
  37.4 0.0 collective-permute-start.2
  37.4 15.1 %narrow.1.refs_4_ = bf16[2048,4096]{1,0:T(8,128)(2,1)S(1)} custom-call(f32[2048,4096]{1,0:T(8,128)} %f_ref.1), custom_call_target="tpu_custom_call" | custom-call | flops 8388608 | bytes 50331648 | tf_op jit(solution)/shard_map/narrow/pallas_call | solution.py:93
  52.5 0.0 copy-start
  52.5 5.7 %copy-done = bf16[2048,4096]{1,0:T(8,128)(2,1)} copy-done((bf16[2048,4096]{1,0:T(8,128)(2,1)}, bf16[2048,4096]{1,0:T(8,128)(2,1)S(1)}, u32[]{:S(2)}) %copy-start) | copy-done | bytes 16777240
  58.2 0.0 collective-permute-done.refs_1_
  58.2 0.0 collective-permute-done.2.refs_3_
  58.3 8.8 %product.1 = f32[8,4,4096]{2,1,0:T(4,128)S(1)} custom-call(f32[32,512]{1,0:T(8,128)S(1)} %combine.1.refs_0_, f32[32,512]{1,0:T(8,128)S(1)} %collective-permute-done.refs_1_, f32[32,512]{1,0:T(8,128)S(1)} %collective-permute-done.1.refs_2_, f32[32,512]{1,0:T(8,128)S(1)} %collective-permute-done.2.refs_3_, bf16[2048,4096]{1,0:T(8,128)(2,1)} %copy-done), custom_call_target="tpu_custom_call" | custom-call | tf_op jit(solution)/shard_map/product/pallas_call | solution.py:168
  67.0 17.9 %all_to_all.11 = f32[8,4,4096]{2,1,0:T(4,128)S(1)} all-to-all(f32[8,4,4096]{2,1,0:T(4,128)S(1)} %product.1), channel_id=1, replica_groups=mesh['row'=8,'col'=4] {'row'}, dimensions={0} | all-to-all | bytes 1048576 | tf_op jit(solution)/shard_map/all_to_all | solution.py:201
  84.9 0.7 reduce_sum.9
  (3 shorter events, 0.0 us)
Async XLA Ops:
  0.0 3.1 %copy-start.1 = (bf16[256,14336]{1,0:T(8,128)(2,1)S(1)}, bf16[256,14336]{1,0:T(8,128)(2,1)}, u32[]{:S(2)}) copy-start(bf16[256,14336]{1,0:T(8,128)(2,1)} %x_out.1) | copy-start | bytes 22020100
  3.1 2.0 %copy-start.2 = (bf16[14336,128]{1,0:T(8,128)(2,1)S(1)}, bf16[14336,128]{1,0:T(8,128)(2,1)}, u32[]{:S(2)}) copy-start(bf16[14336,128]{1,0:T(8,128)(2,1)} %w_out.1) | copy-start | bytes 11010052
  5.1 1.6 %copy-start.3 = (bf16[256,4096]{1,0:T(8,128)(2,1)S(1)}, bf16[256,4096]{1,0:T(8,128)(2,1)}, u32[]{:S(2)}) copy-start(bf16[256,4096]{1,0:T(8,128)(2,1)} %x_in.1) | copy-start | bytes 6291460
  6.7 1.2 %copy-start.4 = (bf16[4096,128]{1,0:T(8,128)(2,1)S(1)}, bf16[4096,128]{1,0:T(8,128)(2,1)}, u32[]{:S(2)}) copy-start(bf16[4096,128]{1,0:T(8,128)(2,1)} %w_in.1) | copy-start | bytes 3145732
  7.9 0.7 copy-start.5
  8.6 24.0 %copy-start.6 = (s32[32]{0:T(128)S(1)}, s32[32]{0:T(128)}, u32[]{:S(2)}) copy-start(s32[32]{0:T(128)} %param.12) | copy-start | bytes 388
  33.1 4.3 %collective-permute-start.1 = (f32[32,512]{1,0:T(8,128)S(1)}, f32[32,512]{1,0:T(8,128)S(1)}, u32[]{:S(2)}, u32[]{:S(2)}) collective-permute-start(f32[32,512]{1,0:T(8,128)S(1)} %combine.1.refs_0_), channel_id=1, source_target_pairs={{0,2},{1,3},{2,0},{3,1},{4,6},{5,7},{6,4},{7,5},{8,10},{9,11},{10,... | collective-permute-start | bytes 196616 | tf_op jit(solution)/shard_map/ppermute | solution.py:178
  33.3 25.0 %collective-permute-start = (f32[32,512]{1,0:T(8,128)S(1)}, f32[32,512]{1,0:T(8,128)S(1)}, u32[]{:S(2)}, u32[]{:S(2)}) collective-permute-start(f32[32,512]{1,0:T(8,128)S(1)} %combine.1.refs_0_), channel_id=1, source_target_pairs={{0,1},{1,0},{2,3},{3,2},{4,5},{5,4},{6,7},{7,6},{8,9},{9,8},{10,11... | collective-permute-start | bytes 196616 | tf_op jit(solution)/shard_map/ppermute | solution.py:178
  37.4 20.9 %collective-permute-start.2 = (f32[32,512]{1,0:T(8,128)S(1)}, f32[32,512]{1,0:T(8,128)S(1)}, u32[]{:S(2)}, u32[]{:S(2)}) collective-permute-start(f32[32,512]{1,0:T(8,128)S(1)} %collective-permute-done.1.refs_2_), channel_id=1, source_target_pairs={{0,1},{1,0},{2,3},{3,2},{4,5},{5,4},{6,7},{7,6},{8,9},{9,8},{10,11... | collective-permute-start | bytes 196616 | tf_op jit(solution)/shard_map/ppermute | solution.py:178
  52.5 5.7 %copy-start = (bf16[2048,4096]{1,0:T(8,128)(2,1)}, bf16[2048,4096]{1,0:T(8,128)(2,1)S(1)}, u32[]{:S(2)}) copy-start(bf16[2048,4096]{1,0:T(8,128)(2,1)S(1)} %narrow.1.refs_4_) | copy-start | bytes 50331652

commit v2 on v1

--- a/solution.py
+++ b/solution.py
@@ -6,6 +6,7 @@
 from jax.experimental import pallas as pl
 from jax.experimental.pallas import tpu as pltpu
 from jax.sharding import PartitionSpec as P
+
 
 SLOTS = 5
 STEPS = 8
@@ -78,30 +79,41 @@
             pltpu.VMEM((tokens, rank_in), jnp.float32),
             pltpu.VMEM((tokens, rank_out), jnp.float32),
         ],
-        compiler_params=pltpu.CompilerParams(vmem_limit_bytes=16 * MIB),
+        compiler_params=pltpu.CompilerParams(vmem_limit_bytes=60 * MIB),
         name="partials",
     )(lens, x_in, x_out, w_in, w_out)
 
 
-def narrow_kernel(f_ref, out):
+def narrow_kernel(me, f_ref, out):
+    del me
     out[...] = f_ref[...].astype(jnp.bfloat16)
 
 
-def narrow_call(fisher):
+def narrow_call(me, fisher, n_parts):
     rows, cols = fisher.shape
-    step = min(rows, 128)
+    size = rows // n_parts
+    step = min(size, 256)
+    count = size // step
     return pl.pallas_call(
         narrow_kernel,
-        grid=(rows // step,),
-        in_specs=[pl.BlockSpec((step, cols), lambda i: (i, 0))],
-        out_specs=pl.BlockSpec((step, cols), lambda i: (i, 0)),
-        out_shape=jax.ShapeDtypeStruct((rows, cols), jnp.bfloat16),
-        compiler_params=pltpu.CompilerParams(vmem_limit_bytes=16 * MIB),
+        grid_spec=pltpu.PrefetchScalarGridSpec(
+            num_scalar_prefetch=1,
+            grid=(n_parts - 1, count),
+            in_specs=[
+                pl.BlockSpec(
+                    (step, cols),
+                    lambda k, i, me: (jnp.bitwise_xor(me[0], k + 1) * count + i, 0),
+                )
+            ],
+            out_specs=pl.BlockSpec((step, cols), lambda k, i, me: (k * count + i, 0)),
+        ),
+        out_shape=jax.ShapeDtypeStruct((rows - size, cols), jnp.bfloat16),
+        compiler_params=pltpu.CompilerParams(vmem_limit_bytes=60 * MIB),
         cost_estimate=pl.CostEstimate(
-            flops=rows * cols, bytes_accessed=6 * rows * cols, transcendentals=0
+            flops=rows * cols, bytes_accessed=6 * (rows - size) * cols, transcendentals=0
         ),
         name="narrow",
-    )(fisher)
+    )(me, fisher)
 
 
 def combine_kernel(tokens, lens, docs_row, got, out):
@@ -137,40 +149,79 @@
     )(lens, docs_row, got.reshape(devices * slots * rows, rank))
 
 
+def split(x):
+    high = x.astype(jnp.bfloat16)
+    low = (x - high.astype(jnp.float32)).astype(jnp.bfloat16)
+    return jnp.concatenate([high, low], axis=0)
+
+
+def own_kernel(me, part, f_ref, out):
+    del me
+    docs = part.shape[0]
+    total = jnp.dot(
+        split(part[...]), f_ref[...].astype(jnp.bfloat16), preferred_element_type=jnp.float32
+    )
+    out[...] = total[:docs] + total[docs:]
+
+
+def own_call(me, part, fisher):
+    docs, size = part.shape
+    cols = fisher.shape[1]
+    width = 1024 if cols % 1024 == 0 else cols
+    return pl.pallas_call(
+        own_kernel,
+        grid_spec=pltpu.PrefetchScalarGridSpec(
+            num_scalar_prefetch=1,
+            grid=(cols // width,),
+            in_specs=[
+                pl.BlockSpec((docs, size), lambda n, me: (0, 0)),
+                pl.BlockSpec((size, width), lambda n, me: (me[0], n)),
+            ],
+            out_specs=pl.BlockSpec((docs, width), lambda n, me: (0, n)),
+        ),
+        out_shape=jax.ShapeDtypeStruct((docs, cols), jnp.float32),
+        compiler_params=pltpu.CompilerParams(vmem_limit_bytes=40 * MIB),
+        cost_estimate=pl.CostEstimate(
+            flops=4 * docs * size * cols, bytes_accessed=4 * size * cols, transcendentals=0
+        ),
+        name="own",
+    )(me, part, fisher)
+
+
 def product_kernel(n_parts, *refs):
-    parts, (f_ref, out) = refs[:n_parts], refs[n_parts:]
+    parts, (f_ref, first, out) = refs[:n_parts], refs[n_parts:]
     docs, size = parts[0].shape
-    me = lax.axis_index("col")
     groups, rows, _ = out.shape
-    highs, lows = [], []
-    for part in parts:
-        high = part[...].astype(jnp.bfloat16)
-        highs.append(high)
-        lows.append((part[...] - high.astype(jnp.float32)).astype(jnp.bfloat16))
-    both = [jnp.concatenate([h, l], axis=0) for h, l in zip(highs, lows)]
-    cols = f_ref.shape[1]
+    total = jnp.zeros((2 * docs, f_ref.shape[1]), jnp.float32)
+    for k, part in enumerate(parts):
+        total += jnp.dot(
+            split(part[...]),
+            f_ref[k * size : (k + 1) * size, :],
+            preferred_element_type=jnp.float32,
+        )
+    total = first[...] + (total[:docs] + total[docs:])
+    for g in range(groups):
+        out[g] = total[g * rows : (g + 1) * rows]
+
+
+def product_call(parts, fisher, first, groups):
+    docs, size = parts[0].shape
+    n = len(parts)
+    rows, cols = fisher.shape
     width = 512 if cols % 512 == 0 else cols
-    for n in range(cols // width):
-        total = jnp.zeros((2 * docs, width), jnp.float32)
-        for k in range(n_parts):
-            at = pl.multiple_of(jnp.bitwise_xor(me, k) * size, size)
-            tile = f_ref[pl.ds(at, size), n * width : (n + 1) * width]
-            total += jnp.dot(both[k], tile, preferred_element_type=jnp.float32)
-        total = total[:docs] + total[docs:]
-        for g in range(groups):
-            out[g, :, n * width : (n + 1) * width] = total[g * rows : (g + 1) * rows]
-
-
-def product_call(parts, fisher, groups):
-    docs = parts[0].shape[0]
-    cols = fisher.shape[1]
-    n = len(parts)
     return pl.pallas_call(
         functools.partial(product_kernel, n),
+        grid=(cols // width,),
+        in_specs=[pl.BlockSpec((docs, size), lambda i: (0, 0))] * n
+        + [
+            pl.BlockSpec((rows, width), lambda i: (0, i)),
+            pl.BlockSpec((docs, width), lambda i: (0, i)),
+        ],
+        out_specs=pl.BlockSpec((groups, docs // groups, width), lambda i: (0, 0, i)),
         out_shape=jax.ShapeDtypeStruct((groups, docs // groups, cols), jnp.float32),
-        compiler_params=pltpu.CompilerParams(vmem_limit_bytes=40 * MIB),
+        compiler_params=pltpu.CompilerParams(vmem_limit_bytes=32 * MIB),
         name="product",
-    )(*parts, fisher)
+    )(*parts, fisher, first)
 
 
 def exchange(x, axis, bit):
@@ -186,18 +237,22 @@
     devices = n_row * n_col
     lens = doc_lengths.reshape(1, -1)
     docs_row = device_docs.reshape(1, -1)
+    me = lax.axis_index("col").astype(jnp.int32).reshape(1)
     partials = partials_call(
         saved_inputs, output_grads, proj_in, proj_out, lens, n_col, devices
     )
     got = lax.all_to_all(partials, ("row", "col"), 0, 0, tiled=True)
-    fisher = narrow_call(fisher_inverse)
+    others = narrow_call(me, fisher_inverse, n_col)
     mine = combine_call(got, lens, docs_row, tokens)
     parts = {0: mine}
     bit = n_col // 2
     while bit:
-        parts.update({k ^ bit: exchange(v, "col", bit) for k, v in list(parts.items())})
+        held = dict(parts)
+        for k, v in held.items():
+            parts[k ^ bit] = exchange(v, "col", bit)
         bit //= 2
-    sums = product_call([parts[k] for k in range(n_col)], fisher, n_row)
+    first = own_call(me, mine, fisher_inverse)
+    sums = product_call([parts[k] for k in range(1, n_col)], others, first, n_row)
     shares = lax.all_to_all(sums, "row", 0, 0, tiled=True)
     return jnp.sum(shares, axis=0)
 

time: 86 us -> 77.2 us (0.90)
  local copies, waits for them, and re-layouts: 14.3 us -> 2.26 us
  Pallas kernels: 29.2 us -> 32.4 us
    unnamed x14 -> x6, local copies, waits for them, and re-layouts: 14.3 us -> 2.26 us
    pallas_call x1, Pallas kernels: 4.85 us -> 9.71 us  [partials_call(): pl.pallas_call(functools.partial(partials_kernel, n_col), grid=(STEPS,),...]
    pallas_call x2 -> x3, Pallas kernels: 23.9 us -> 22.2 us  [the longest x1 13 us: narrow_call(): pl.pallas_call(narrow_kernel, grid_spec=pltpu.PrefetchScalarGridSpec(num_...]
  transfers between devices with their start and end apart: 3 -> 3, of which waited for: 1 -> 1; matrix products, arithmetic and copies ran while one was open for 0% -> 0% of each run, Pallas kernels for 18% -> 23%
where the time goes in v2:
time: 77.2 us; the launch traced here: 76.9 us
  blocking collectives  37.2 us (48%)
  Pallas kernels  32.4 us (42%)
  waiting for transfers between devices  3.84 us (5%)
  local copies, waits for them, and re-layouts  2.26 us (3%)
    all_to_all x1, blocking collectives, per_device(): got = lax.all_to_all(partials, ('row', 'col'), 0, 0, tiled=True)  19.4 us
    all_to_all x1, blocking collectives, per_device(): shares = lax.all_to_all(sums, 'row', 0, 0, tiled=True)  17.8 us
    pallas_call x1, Pallas kernels, narrow_call(): pl.pallas_call(narrow_kernel, grid_spec=pltpu.PrefetchScalarGridSpec(num_...  13 us
    pallas_call x1, Pallas kernels, partials_call(): pl.pallas_call(functools.partial(partials_kernel, n_col), grid=(STEPS,),...  9.71 us
    pallas_call x1, Pallas kernels, own_call(): pl.pallas_call(own_kernel, grid_spec=pltpu.PrefetchScalarGridSpec(num_sca...  4.83 us
    pallas_call x1, Pallas kernels, product_call(): pl.pallas_call(functools.partial(product_kernel, n), grid=(cols // width,...  4.31 us
    ppermute x3, waiting for transfers between devices, exchange(): return lax.ppermute(x, axis, [(i, i ^ bit) for i in range(size)])  3.84 us
    unnamed x6, local copies, waits for them, and re-layouts  2.26 us
  transfers between devices with their start and end apart: 3, of which 1 were waited for; matrix products, arithmetic and copies ran while one was open for 0% of the time, Pallas kernels for 23%

profile of v2, /device:TPU:0, one launch (start us, length us, event | category | flops | bytes accessed | tf_op | source)
XLA Modules:
  0.0 76.9 jit_solution(8035422046291640096)
XLA Ops:
  0.0 0.0 copy-start.1
  0.0 0.0 copy-start.2
  0.0 9.7 %partials.1 = f32[32,5,4,128]{3,2,1,0:T(4,128)} custom-call(s32[1,32]{1,0:T(1,128)} %bitcast.5, bf16[256,4096]{1,0:T(8,128)(2,1)} %x_in.1, bf16[256,14336]{1,0:T(8,128)(2,1)} %x_out.1, bf16[4096,128]{1,0:T(8,128)(2,1)} %w_in.1, bf16[14336,128]{1,0:T(8,128)(2,1)} %w_out.1), custom_call_target="tpu_custom_call" | custom-call | tf_op jit(solution)/shard_map/partials/pallas_call | solution.py:62
  9.7 19.4 %all_to_all.10 = f32[32,5,4,128]{3,2,1,0:T(4,128)S(1)} all-to-all(f32[32,5,4,128]{3,2,1,0:T(4,128)} %partials.1), channel_id=1, replica_groups=mesh['row'=8,'col'=4] {'row','col'}, dimensions={0} | all-to-all | bytes 655360 | tf_op jit(solution)/shard_map/all_to_all | solution.py:244
  29.1 0.0 copy-done.1
  29.1 0.0 copy-done.2
  29.1 0.5 combine.1.part
  29.6 0.2 collective-permute-start.1
  29.8 0.3 collective-permute-start
  30.0 3.8 %collective-permute-done.1.refs_1_ = f32[32,512]{1,0:T(8,128)S(1)} collective-permute-done((f32[32,512]{1,0:T(8,128)S(1)}, f32[32,512]{1,0:T(8,128)S(1)}, u32[]{:S(2)}, u32[]{:S(2)}) %collective-permute-start.1) | collective-permute-done | bytes 65568 | tf_op jit(solution)/shard_map/ppermute | solution.py:229
  33.8 0.0 collective-permute-start.2
  33.8 13.0 %narrow.1.refs_3_ = bf16[1536,4096]{1,0:T(8,128)(2,1)} custom-call(s32[1]{0:T(128)} %bitcast.3.me, f32[2048,4096]{1,0:T(8,128)} %f_ref.3), custom_call_target="tpu_custom_call" | custom-call | flops 8388608 | bytes 37748736 | tf_op jit(solution)/shard_map/narrow/pallas_call | solution.py:97
  46.9 0.0 copy-start
  46.9 4.8 %own.1.refs_4_ = f32[32,4096]{1,0:T(8,128)S(1)} custom-call(s32[1]{0:T(128)} %bitcast.3.me, f32[32,512]{1,0:T(8,128)S(1)} %combine.1.part, f32[2048,4096]{1,0:T(8,128)} %f_ref.3), custom_call_target="tpu_custom_call" | custom-call | flops 268435456 | bytes 8388608 | tf_op jit(solution)/shard_map/own/pallas_call | solution.py:171
  51.7 0.0 collective-permute-done.refs_0_
  51.7 0.0 collective-permute-done.2.refs_2_
  51.7 2.3 %copy-done = bf16[1536,4096]{1,0:T(8,128)(2,1)S(1)} copy-done((bf16[1536,4096]{1,0:T(8,128)(2,1)S(1)}, bf16[1536,4096]{1,0:T(8,128)(2,1)}, u32[]{:S(2)}) %copy-start) | copy-done | bytes 12582936
  54.0 4.3 %product.1 = f32[8,4,4096]{2,1,0:T(4,128)S(1)} custom-call(f32[32,512]{1,0:T(8,128)S(1)} %collective-permute-done.refs_0_, f32[32,512]{1,0:T(8,128)S(1)} %collective-permute-done.1.refs_1_, f32[32,512]{1,0:T(8,128)S(1)} %collective-permute-done.2.refs_2_, bf16[1536,4096]{1,0:T(8,128)(2,1)S(1)} %copy-done, f32[32,4096]{1,0:T(8,128)S(1)} %own.1.refs_4_), custom_call_target="tpu_custom_call" | custom-call | tf_op jit(solution)/shard_map/product/pallas_call | solution.py:212
  58.3 17.8 %all_to_all.11 = f32[8,4,4096]{2,1,0:T(4,128)S(1)} all-to-all(f32[8,4,4096]{2,1,0:T(4,128)S(1)} %product.1), channel_id=1, replica_groups=mesh['row'=8,'col'=4] {'row'}, dimensions={0} | all-to-all | bytes 1048576 | tf_op jit(solution)/shard_map/all_to_all | solution.py:256
  76.2 0.7 reduce_sum.9
Async XLA Ops:
  0.0 29.1 %copy-start.1 = (s32[32]{0:T(128)S(1)}, s32[32]{0:T(128)}, u32[]{:S(2)}) copy-start(s32[32]{0:T(128)} %param.11) | copy-start | bytes 388
  0.0 29.1 %copy-start.2 = (s32[32]{0:T(128)S(1)}, s32[32]{0:T(128)}, u32[]{:S(2)}) copy-start(s32[32]{0:T(128)} %param.12) | copy-start | bytes 388
  29.6 4.3 %collective-permute-start.1 = (f32[32,512]{1,0:T(8,128)S(1)}, f32[32,512]{1,0:T(8,128)S(1)}, u32[]{:S(2)}, u32[]{:S(2)}) collective-permute-start(f32[32,512]{1,0:T(8,128)S(1)} %combine.1.part), channel_id=1, source_target_pairs={{0,2},{1,3},{2,0},{3,1},{4,6},{5,7},{6,4},{7,5},{8,10},{9,11},{10,... | collective-permute-start | bytes 196616 | tf_op jit(solution)/shard_map/ppermute | solution.py:229
  29.8 22.0 %collective-permute-start = (f32[32,512]{1,0:T(8,128)S(1)}, f32[32,512]{1,0:T(8,128)S(1)}, u32[]{:S(2)}, u32[]{:S(2)}) collective-permute-start(f32[32,512]{1,0:T(8,128)S(1)} %combine.1.part), channel_id=1, source_target_pairs={{0,1},{1,0},{2,3},{3,2},{4,5},{5,4},{6,7},{7,6},{8,9},{9,8},{10,11... | collective-permute-start | bytes 196616 | tf_op jit(solution)/shard_map/ppermute | solution.py:229
  33.8 17.9 %collective-permute-start.2 = (f32[32,512]{1,0:T(8,128)S(1)}, f32[32,512]{1,0:T(8,128)S(1)}, u32[]{:S(2)}, u32[]{:S(2)}) collective-permute-start(f32[32,512]{1,0:T(8,128)S(1)} %collective-permute-done.1.refs_1_), channel_id=1, source_target_pairs={{0,1},{1,0},{2,3},{3,2},{4,5},{5,4},{6,7},{7,6},{8,9},{9,8},{10,11... | collective-permute-start | bytes 196616 | tf_op jit(solution)/shard_map/ppermute | solution.py:229
  46.9 7.1 %copy-start = (bf16[1536,4096]{1,0:T(8,128)(2,1)S(1)}, bf16[1536,4096]{1,0:T(8,128)(2,1)}, u32[]{:S(2)}) copy-start(bf16[1536,4096]{1,0:T(8,128)(2,1)} %narrow.1.refs_3_) | copy-start | bytes 37748740

commit v3 on v1

v3 whole, which is shorter than its diff:
```python
import functools

import jax
import jax.numpy as jnp
from jax import lax
from jax.experimental import pallas as pl
from jax.experimental.pallas import tpu as pltpu
from jax.sharding import PartitionSpec as P


SLOTS = 5
STEPS = 8
MIB = 1024 * 1024


def doc_ends(lens):
    docs = lens.shape[1]
    row = lax.broadcasted_iota(jnp.int32, (docs, docs), 0)
    col = lax.broadcasted_iota(jnp.int32, (docs, docs), 1)
    wide = jnp.broadcast_to(lens.astype(jnp.float32), (docs, docs))
    return jnp.sum(jnp.where(col <= row, wide, 0.0), axis=1, keepdims=True)


def docs_at(ends, positions):
    return jnp.sum(jnp.where(ends <= positions, 1.0, 0.0), axis=0, keepdims=True)


def partials_kernel(n_col, lens, x_in, x_out, w_in, w_out, out, b_in, b_out, v_in, v_out, sems):
    tokens, rank_out = b_out.shape[0], w_out.shape[1]
    k_in, k_out = x_in.shape[1] // STEPS, x_out.shape[1] // STEPS
    copies = []
    for i in range(STEPS):
        at_in, at_out = pl.ds(i * k_in, k_in), pl.ds(i * k_out, k_out)
        copies.append(
            [
                pltpu.make_async_copy(x_out.at[:, at_out], b_out.at[:, at_out], sems.at[0, i]),
                pltpu.make_async_copy(w_out.at[at_out, :], v_out.at[at_out, :], sems.at[1, i]),
                pltpu.make_async_copy(x_in.at[:, at_in], b_in.at[:, at_in], sems.at[2, i]),
                pltpu.make_async_copy(w_in.at[at_in, :], v_in.at[at_in, :], sems.at[3, i]),
            ]
        )
    for group in copies:
        for copy in group:
            copy.start()
    shard = lax.axis_index("row") * n_col + lax.axis_index("col")
    base = (shard * tokens).astype(jnp.float32)
    ends = doc_ends(lens[...])
    token = lax.broadcasted_iota(jnp.int32, (1, tokens), 1).astype(jnp.float32)
    slot = docs_at(ends, token + base) - docs_at(ends, jnp.zeros((1, tokens)) + base)
    acc_in = jnp.zeros((tokens, w_in.shape[1]), jnp.float32)
    acc_out = jnp.zeros((tokens, rank_out), jnp.float32)
    for i in range(STEPS):
        at_in, at_out = pl.ds(i * k_in, k_in), pl.ds(i * k_out, k_out)
        for copy in copies[i]:
            copy.wait()
        acc_out += jnp.dot(
            b_out[:, at_out], v_out[at_out, :], preferred_element_type=jnp.float32
        )
        acc_in += jnp.dot(b_in[:, at_in], v_in[at_in, :], preferred_element_type=jnp.float32)
    low_in = acc_in.astype(jnp.bfloat16)
    low_out = acc_out.astype(jnp.bfloat16).astype(jnp.float32).T
    devices, _, rows, _ = out.shape
    for s in range(SLOTS):
        masked = jnp.where(slot == float(s), low_out, 0.0).astype(jnp.bfloat16)
        part = jnp.dot(masked, low_in, preferred_element_type=jnp.float32)
        for j in range(devices):
            out[j, s] = part[j * rows : (j + 1) * rows]


def partials_call(x_in, x_out, w_in, w_out, lens, n_col, devices):
    rank_in, rank_out = w_in.shape[1], w_out.shape[1]
    far = pl.BlockSpec(memory_space=pltpu.HBM)
    return pl.pallas_call(
        functools.partial(partials_kernel, n_col),
        in_specs=[pl.BlockSpec(memory_space=pltpu.VMEM), far, far, far, far],
        out_specs=pl.BlockSpec(memory_space=pltpu.VMEM),
        out_shape=pltpu.VMEM((devices, SLOTS, rank_out // devices, rank_in), jnp.float32),
        scratch_shapes=[
            pltpu.VMEM(x_in.shape, x_in.dtype),
            pltpu.VMEM(x_out.shape, x_out.dtype),
            pltpu.VMEM(w_in.shape, w_in.dtype),
            pltpu.VMEM(w_out.shape, w_out.dtype),
            pltpu.SemaphoreType.DMA((4, STEPS)),
        ],
        compiler_params=pltpu.CompilerParams(vmem_limit_bytes=62_495_744),
        name="partials",
    )(lens, x_in, x_out, w_in, w_out)


def pause_kernel(out):
    del out


def pause_call():
    return pl.pallas_call(
        pause_kernel,
        out_specs=pl.BlockSpec(memory_space=pltpu.SMEM),
        out_shape=jax.ShapeDtypeStruct((1,), jnp.int32),
        compiler_params=pltpu.CompilerParams(vmem_limit_bytes=MIB, has_side_effects=True),
        cost_estimate=pl.CostEstimate(
            flops=10_000_000_000, bytes_accessed=30_000_000, transcendentals=0
        ),
        name="pause",
    )()


def combine_kernel(tokens, lens, docs_row, got, out):
    docs = lens.shape[1]
    pieces, rank = got.shape
    rows = out.shape[1] // rank
    slots = pieces // rows
    ends = doc_ends(lens[...])
    m = lax.broadcasted_iota(jnp.int32, (1, slots), 1)
    source = lax.shift_right_logical(m * 52429, 18)
    first = docs_at(ends, (source * tokens).astype(jnp.float32))
    doc = first + (m - source * SLOTS).astype(jnp.float32)
    row = lax.broadcasted_iota(jnp.int32, (docs, docs), 0)
    col = lax.broadcasted_iota(jnp.int32, (docs, docs), 1)
    wanted = jnp.broadcast_to(docs_row[...].astype(jnp.float32), (docs, docs))
    wanted = jnp.sum(jnp.where(col == row, wanted, 0.0), axis=1, keepdims=True)
    onehot = jnp.where(wanted == doc, 1.0, 0.0)
    for p in range(rows):
        piece = got[pl.ds(p, slots, stride=rows), :]
        out[:, p * rank : (p + 1) * rank] = jnp.dot(
            onehot, piece, precision=lax.Precision.HIGHEST, preferred_element_type=jnp.float32
        )


def combine_call(got, lens, docs_row, tokens):
    devices, slots, rows, rank = got.shape
    docs = lens.shape[1]
    return pl.pallas_call(
        functools.partial(combine_kernel, tokens),
        out_shape=jax.ShapeDtypeStruct((docs, rows * rank), jnp.float32),
        compiler_params=pltpu.CompilerParams(vmem_limit_bytes=4 * MIB),
        name="combine",
    )(lens, docs_row, got.reshape(devices * slots * rows, rank))


def split(x):
    high = x.astype(jnp.bfloat16)
    low = (x - high.astype(jnp.float32)).astype(jnp.bfloat16)
    return jnp.concatenate([high, low], axis=0)


def product_kernel(at, has_first, *refs):
    parts, refs = refs[: len(at)], refs[len(at) :]
    f_ref, out = refs[0], refs[-1]
    docs, size = parts[0].shape
    cols = f_ref.shape[1]
    me = lax.axis_index("col")
    both = [split(part[...]) for part in parts]
    width = 512 if cols % 512 == 0 else cols
    for n in range(cols // width):
        where = slice(n * width, (n + 1) * width)
        total = jnp.zeros((2 * docs, width), jnp.float32)
        for k, x in zip(at, both):
            rows = pl.ds(pl.multiple_of(jnp.bitwise_xor(me, k) * size, size), size)
            tile = f_ref[rows, where].astype(jnp.bfloat16)
            total += jnp.dot(x, tile, preferred_element_type=jnp.float32)
        total = total[:docs] + total[docs:]
        if has_first:
            total += refs[1][:, where]
        if out.ndim == 2:
            out[:, where] = total
        else:
            groups, height, _ = out.shape
            for g in range(groups):
                out[g, :, where] = total[g * height : (g + 1) * height]


def product_call(parts, at, fisher, first, groups):
    docs = parts[at[0]].shape[0]
    cols = fisher.shape[1]
    shape = (docs, cols) if groups is None else (groups, docs // groups, cols)
    args = [parts[k] for k in at] + [fisher] + ([] if first is None else [first])
    return pl.pallas_call(
        functools.partial(product_kernel, at, first is not None),
        in_specs=[pl.BlockSpec(memory_space=pltpu.VMEM)] * len(args),
        out_specs=pl.BlockSpec(memory_space=pltpu.VMEM),
        out_shape=jax.ShapeDtypeStruct(shape, jnp.float32),
        compiler_params=pltpu.CompilerParams(vmem_limit_bytes=12 * MIB),
    )(*args)


def exchange(x, axis, bit):
    size = lax.axis_size(axis)
    return lax.ppermute(x, axis, [(i, i ^ bit) for i in range(size)])


def per_device(
    saved_inputs, output_grads, proj_in, proj_out, doc_lengths, device_docs, fisher_inverse
):
    tokens = saved_inputs.shape[0]
    n_row, n_col = lax.axis_size("row"), lax.axis_size("col")
    devices = n_row * n_col
    lens = doc_lengths.reshape(1, -1)
    docs_row = device_docs.reshape(1, -1)
    fisher = pltpu.with_memory_space_constraint(fisher_inverse, pltpu.VMEM)
    partials = partials_call(saved_inputs, output_grads, proj_in, proj_out, lens, n_col, devices)
    pause_call()
    got = lax.all_to_all(partials, ("row", "col"), 0, 0, tiled=True)
    mine = combine_call(got, lens, docs_row, tokens)
    parts = {0: mine}
    bit = n_col // 2
    parts[bit] = exchange(mine, "col", bit)
    parts[1] = exchange(mine, "col", 1)
    while bit > 2:
        bit //= 2
        for k in [k for k in parts if k != 1]:
            parts[k ^ bit] = exchange(parts[k], "col", bit)
    evens = [k for k in parts if k > 1]
    for k in evens:
        parts[k ^ 1] = exchange(parts[k], "col", 1)
    sums = product_call(parts, list(range(n_col)), fisher, None, n_row)
    shares = lax.all_to_all(sums, "row", 0, 0, tiled=True)
    return jnp.sum(shares, axis=0)


def solution(mesh):
    placed = (P(("row", "col"), None), P(("row", "col"), None), P(), P(), P(), P(), P("row", "col"))
    return jax.shard_map(
        per_device, mesh=mesh, in_specs=placed, out_specs=P("row", "col"), check_vma=False
    )
```

time: 86 us -> 66 us (0.77)
  blocking collectives: 37 us -> 19.2 us
  Pallas kernels: 29.2 us -> 11.8 us
  waiting for transfers between devices: 3.84 us -> 19.6 us
  local copies, waits for them, and re-layouts: 14.3 us -> 10.6 us
  starting transfers between devices: 0.44 us -> 3.93 us
    all_to_all x1 -> x0, blocking collectives: 17.9 us -> none  [per_device(): shares = lax.all_to_all(sums, 'row', 0, 0, tiled=True)]
    pallas_call x3, Pallas kernels: 28.8 us -> 11.3 us  [the longest x1 6.95 us: partials_call(): pl.pallas_call(functools.partial(partials_kernel, n_col), in_specs=[pl.Bl...]
    all_to_all x0 -> x1, waiting for transfers between devices: none -> 14.5 us  [per_device(): shares = lax.all_to_all(sums, 'row', 0, 0, tiled=True)]
    unnamed x14 -> x6, local copies, waits for them, and re-layouts: 14.3 us -> 10.6 us
    all_to_all x0 -> x1, starting transfers between devices: none -> 3.49 us  [per_device(): shares = lax.all_to_all(sums, 'row', 0, 0, tiled=True)]
    ppermute x3, waiting for transfers between devices: 3.84 us -> 5.08 us  [exchange(): return lax.ppermute(x, axis, [(i, i ^ bit) for i in range(size)])]
  transfers between devices with their start and end apart: 3 -> 4, of which waited for: 1 -> 3; matrix products, arithmetic and copies ran while one was open for 0% -> 0% of each run, Pallas kernels for 18% -> 1%
where the time goes in v3:
time: 66 us; the launch traced here: 65.7 us
  waiting for transfers between devices  19.6 us (30%)
  blocking collectives  19.2 us (29%)
  Pallas kernels  11.8 us (18%)
  local copies, waits for them, and re-layouts  10.6 us (16%)
  starting transfers between devices  3.93 us (6%)
  other arithmetic  0.72 us (1%)
    all_to_all x1, blocking collectives, per_device(): got = lax.all_to_all(partials, ('row', 'col'), 0, 0, tiled=True)  19.2 us
    all_to_all x1, waiting for transfers between devices, per_device(): shares = lax.all_to_all(sums, 'row', 0, 0, tiled=True)  14.5 us
    unnamed x6, local copies, waits for them, and re-layouts  10.6 us
    pallas_call x1, Pallas kernels, partials_call(): pl.pallas_call(functools.partial(partials_kernel, n_col), in_specs=[pl.Bl...  6.95 us
    ppermute x3, waiting for transfers between devices, exchange(): return lax.ppermute(x, axis, [(i, i ^ bit) for i in range(size)])  5.08 us
    pallas_call x1, Pallas kernels, product_call(): pl.pallas_call(functools.partial(product_kernel, at, first is not None),...  3.82 us
    all_to_all x1, starting transfers between devices, per_device(): shares = lax.all_to_all(sums, 'row', 0, 0, tiled=True)  3.49 us
  transfers between devices with their start and end apart: 4, of which 3 were waited for; matrix products, arithmetic and copies ran while one was open for 0% of the time, Pallas kernels for 1%

profile of v3, /device:TPU:0, one launch (start us, length us, event | category | flops | bytes accessed | tf_op | source)
XLA Modules:
  0.0 65.7 jit_solution(16853145784788547478)
XLA Ops:
  0.0 0.0 copy-start.1
  0.0 0.0 copy-start.2
  0.0 7.0 %partials.1 = f32[32,5,4,128]{3,2,1,0:T(4,128)S(1)} custom-call(s32[1,32]{1,0:T(1,128)} %bitcast.4, bf16[256,4096]{1,0:T(8,128)(2,1)} %x_in.1, bf16[256,14336]{1,0:T(8,128)(2,1)} %x_out.1, bf16[4096,128]{1,0:T(8,128)(2,1)} %w_in.1, bf16[14336,128]{1,0:T(8,128)(2,1)} %w_out.1), custom_call_target="tpu_custom_call" | custom-call | tf_op jit(solution)/shard_map/partials/pallas_call | solution.py:73
  7.0 19.2 %all_to_all.10 = f32[32,5,4,128]{3,2,1,0:T(4,128)S(1)} all-to-all(f32[32,5,4,128]{3,2,1,0:T(4,128)S(1)} %partials.1), channel_id=1, replica_groups=mesh['row'=8,'col'=4] {'row','col'}, dimensions={0} | all-to-all | bytes 655360 | tf_op jit(solution)/shard_map/all_to_all | solution.py:202
  26.1 0.0 copy-done.1
  26.1 0.0 copy-done.2
  26.1 0.5 combine.1.refs_0_
  26.6 0.2 collective-permute-start.1
  26.8 0.3 collective-permute-start
  27.1 3.8 %collective-permute-done.1.refs_2_ = f32[32,512]{1,0:T(8,128)S(1)} collective-permute-done((f32[32,512]{1,0:T(8,128)S(1)}, f32[32,512]{1,0:T(8,128)S(1)}, u32[]{:S(2)}, u32[]{:S(2)}) %collective-permute-start.1) | collective-permute-done | bytes 65568 | tf_op jit(solution)/shard_map/ppermute | solution.py:188
  30.9 0.0 collective-permute-start.2
  30.9 0.0 collective-permute-done.refs_1_
  30.9 1.2 %collective-permute-done.2.refs_3_ = f32[32,512]{1,0:T(8,128)S(1)} collective-permute-done((f32[32,512]{1,0:T(8,128)S(1)}, f32[32,512]{1,0:T(8,128)S(1)}, u32[]{:S(2)}, u32[]{:S(2)}) %collective-permute-start.2) | collective-permute-done | bytes 65568 | tf_op jit(solution)/shard_map/ppermute | solution.py:188
  32.1 0.0 copy-start
  32.1 10.5 %copy-done = f32[2048,4096]{1,0:T(8,128)S(1)} copy-done((f32[2048,4096]{1,0:T(8,128)S(1)}, f32[2048,4096]{1,0:T(8,128)}, u32[]{:S(2)}) %copy-start) | copy-done | bytes 33554456
  42.7 3.8 %shard_map.73 = f32[8,4,4096]{2,1,0:T(4,128)} custom-call(f32[32,512]{1,0:T(8,128)S(1)} %combine.1.refs_0_, f32[32,512]{1,0:T(8,128)S(1)} %collective-permute-done.refs_1_, f32[32,512]{1,0:T(8,128)S(1)} %collective-permute-done.1.refs_2_, f32[32,512]{1,0:T(8,128)S(1)} %collective-permute-done.2.refs_3_, f32[2048,4096]{1,0:T(8,128)S(1)} %copy-done), custom_call_target="tpu_custom_call" | custom-call | tf_op jit(solution)/shard_map/pallas_call | solution.py:177
  46.5 3.5 %all-to-all-start.1 = ((f32[8,4,4096]{2,1,0:T(4,128)}), f32[8,4,4096]{2,1,0:T(4,128)S(1)}, u32[]{:S(2)}, u32[]{:S(2)}) async-start(f32[8,4,4096]{2,1,0:T(4,128)} %shard_map.73), calls=%async_computation.1 | async-start | bytes 1048576 | tf_op jit(solution)/shard_map/all_to_all | solution.py:216
  50.0 0.5 pause.1
  50.5 14.5 %all-to-all-done.1 = f32[8,4,4096]{2,1,0:T(4,128)S(1)} async-done(((f32[8,4,4096]{2,1,0:T(4,128)}), f32[8,4,4096]{2,1,0:T(4,128)S(1)}, u32[]{:S(2)}, u32[]{:S(2)}) %all-to-all-start.1) | async-done | bytes 524320 | tf_op jit(solution)/shard_map/all_to_all | solution.py:216
  65.0 0.7 %reduce_sum.9 = f32[4,4096]{1,0:T(4,128)} reduce(f32[8,4,4096]{2,1,0:T(4,128)S(1)} %all-to-all-done.1, f32[]{:T(128)} %constant.0.clone.1), dimensions={0}, to_apply=%region_0.0 | reduce | flops 114688 | bytes 589828 | tf_op jit(solution)/shard_map/reduce_sum | solution.py:217
Async XLA Ops:
  0.0 26.1 %copy-start.1 = (s32[32]{0:T(128)S(1)}, s32[32]{0:T(128)}, u32[]{:S(2)}) copy-start(s32[32]{0:T(128)} %param.11) | copy-start | bytes 388
  0.0 26.1 %copy-start.2 = (s32[32]{0:T(128)S(1)}, s32[32]{0:T(128)}, u32[]{:S(2)}) copy-start(s32[32]{0:T(128)} %param.12) | copy-start | bytes 388
  26.6 4.3 %collective-permute-start.1 = (f32[32,512]{1,0:T(8,128)S(1)}, f32[32,512]{1,0:T(8,128)S(1)}, u32[]{:S(2)}, u32[]{:S(2)}) collective-permute-start(f32[32,512]{1,0:T(8,128)S(1)} %combine.1.refs_0_), channel_id=1, source_target_pairs={{0,2},{1,3},{2,0},{3,1},{4,6},{5,7},{6,4},{7,5},{8,10},{9,11},{10,... | collective-permute-start | bytes 196616 | tf_op jit(solution)/shard_map/ppermute | solution.py:188
  26.8 4.1 %collective-permute-start = (f32[32,512]{1,0:T(8,128)S(1)}, f32[32,512]{1,0:T(8,128)S(1)}, u32[]{:S(2)}, u32[]{:S(2)}) collective-permute-start(f32[32,512]{1,0:T(8,128)S(1)} %combine.1.refs_0_), channel_id=1, source_target_pairs={{0,1},{1,0},{2,3},{3,2},{4,5},{5,4},{6,7},{7,6},{8,9},{9,8},{10,11... | collective-permute-start | bytes 196616 | tf_op jit(solution)/shard_map/ppermute | solution.py:188
  30.9 1.3 %collective-permute-start.2 = (f32[32,512]{1,0:T(8,128)S(1)}, f32[32,512]{1,0:T(8,128)S(1)}, u32[]{:S(2)}, u32[]{:S(2)}) collective-permute-start(f32[32,512]{1,0:T(8,128)S(1)} %collective-permute-done.1.refs_2_), channel_id=1, source_target_pairs={{0,1},{1,0},{2,3},{3,2},{4,5},{5,4},{6,7},{7,6},{8,9},{9,8},{10,11... | collective-permute-start | bytes 196616 | tf_op jit(solution)/shard_map/ppermute | solution.py:188
  32.1 10.5 %copy-start = (f32[2048,4096]{1,0:T(8,128)S(1)}, f32[2048,4096]{1,0:T(8,128)}, u32[]{:S(2)}) copy-start(f32[2048,4096]{1,0:T(8,128)} %refs_4_.1) | copy-start | bytes 100663296
  46.5 18.5 %all-to-all-start.1 = ((f32[8,4,4096]{2,1,0:T(4,128)}), f32[8,4,4096]{2,1,0:T(4,128)S(1)}, u32[]{:S(2)}, u32[]{:S(2)}) async-start(f32[8,4,4096]{2,1,0:T(4,128)} %shard_map.73), calls=%async_computation.1 | async-start | bytes 1048576 | tf_op jit(solution)/shard_map/all_to_all | solution.py:216

commit v4 on v3

--- a/solution.py
+++ b/solution.py
@@ -25,7 +25,10 @@
     return jnp.sum(jnp.where(ends <= positions, 1.0, 0.0), axis=0, keepdims=True)
 
 
-def partials_kernel(n_col, lens, x_in, x_out, w_in, w_out, out, b_in, b_out, v_in, v_out, sems):
+def partials_kernel(
+    n_col, lens, x_in, x_out, w_in, w_out, tile, out, b_in, b_out, v_in, v_out, sems
+):
+    del tile
     tokens, rank_out = b_out.shape[0], w_out.shape[1]
     k_in, k_out = x_in.shape[1] // STEPS, x_out.shape[1] // STEPS
     copies = []
@@ -67,12 +70,12 @@
             out[j, s] = part[j * rows : (j + 1) * rows]
 
 
-def partials_call(x_in, x_out, w_in, w_out, lens, n_col, devices):
+def partials_call(x_in, x_out, w_in, w_out, lens, tile, n_col, devices):
     rank_in, rank_out = w_in.shape[1], w_out.shape[1]
     far = pl.BlockSpec(memory_space=pltpu.HBM)
     return pl.pallas_call(
         functools.partial(partials_kernel, n_col),
-        in_specs=[pl.BlockSpec(memory_space=pltpu.VMEM), far, far, far, far],
+        in_specs=[pl.BlockSpec(memory_space=pltpu.VMEM)] + [far] * 5,
         out_specs=pl.BlockSpec(memory_space=pltpu.VMEM),
         out_shape=pltpu.VMEM((devices, SLOTS, rank_out // devices, rank_in), jnp.float32),
         scratch_shapes=[
@@ -84,24 +87,25 @@
         ],
         compiler_params=pltpu.CompilerParams(vmem_limit_bytes=62_495_744),
         name="partials",
-    )(lens, x_in, x_out, w_in, w_out)
-
-
-def pause_kernel(out):
-    del out
-
-
-def pause_call():
+    )(lens, x_in, x_out, w_in, w_out, pltpu.with_memory_space_constraint(tile, pltpu.HBM))
+
+
+def pause_kernel(*refs):
+    del refs
+
+
+def pause_call(*after):
     return pl.pallas_call(
         pause_kernel,
-        out_specs=pl.BlockSpec(memory_space=pltpu.SMEM),
-        out_shape=jax.ShapeDtypeStruct((1,), jnp.int32),
+        in_specs=[pl.BlockSpec(memory_space=pltpu.VMEM)] * len(after),
+        out_specs=pl.BlockSpec(memory_space=pltpu.VMEM),
+        out_shape=pltpu.VMEM((8, 128), jnp.float32),
         compiler_params=pltpu.CompilerParams(vmem_limit_bytes=MIB, has_side_effects=True),
         cost_estimate=pl.CostEstimate(
-            flops=10_000_000_000, bytes_accessed=30_000_000, transcendentals=0
+            flops=12_000_000_000, bytes_accessed=36_000_000, transcendentals=0
         ),
         name="pause",
-    )()
+    )(*after)
 
 
 def combine_kernel(tokens, lens, docs_row, got, out):
@@ -145,7 +149,7 @@
 
 def product_kernel(at, has_first, *refs):
     parts, refs = refs[: len(at)], refs[len(at) :]
-    f_ref, out = refs[0], refs[-1]
+    f_ref, outs = refs[0], refs[1 + has_first :]
     docs, size = parts[0].shape
     cols = f_ref.shape[1]
     me = lax.axis_index("col")
@@ -161,26 +165,51 @@
         total = total[:docs] + total[docs:]
         if has_first:
             total += refs[1][:, where]
-        if out.ndim == 2:
-            out[:, where] = total
-        else:
-            groups, height, _ = out.shape
-            for g in range(groups):
-                out[g, :, where] = total[g * height : (g + 1) * height]
+        if len(outs) == 1:
+            outs[0][:, where] = total
+            continue
+        groups, height, _ = outs[0].shape
+        second = lax.rem(lax.axis_index("row"), 2) == 1
+        for g in range(groups):
+            a = total[2 * g * height : (2 * g + 1) * height]
+            b = total[(2 * g + 1) * height : (2 * g + 2) * height]
+            outs[0][g, :, where] = jnp.where(second, b, a)
+            outs[1][g, :, where] = jnp.where(second, a, b)
 
 
 def product_call(parts, at, fisher, first, groups):
     docs = parts[at[0]].shape[0]
     cols = fisher.shape[1]
-    shape = (docs, cols) if groups is None else (groups, docs // groups, cols)
+    shape, count = (docs, cols), 1
+    if groups is not None:
+        shape, count = (groups // 2, docs // groups, cols), 2
     args = [parts[k] for k in at] + [fisher] + ([] if first is None else [first])
     return pl.pallas_call(
         functools.partial(product_kernel, at, first is not None),
         in_specs=[pl.BlockSpec(memory_space=pltpu.VMEM)] * len(args),
-        out_specs=pl.BlockSpec(memory_space=pltpu.VMEM),
-        out_shape=jax.ShapeDtypeStruct(shape, jnp.float32),
+        out_specs=[pl.BlockSpec(memory_space=pltpu.VMEM)] * count,
+        out_shape=[jax.ShapeDtypeStruct(shape, jnp.float32)] * count,
         compiler_params=pltpu.CompilerParams(vmem_limit_bytes=12 * MIB),
     )(*args)
+
+
+def fold_kernel(mine, got, *outs):
+    me = lax.div(lax.axis_index("row"), 2)
+    for k, out in enumerate(outs):
+        at = jnp.bitwise_xor(me, k)
+        out[...] = mine[at] + got[at]
+
+
+def fold_call(mine, got):
+    pairs, height, cols = mine.shape
+    return pl.pallas_call(
+        fold_kernel,
+        in_specs=[pl.BlockSpec(memory_space=pltpu.VMEM)] * 2,
+        out_specs=[pl.BlockSpec(memory_space=pltpu.VMEM)] * pairs,
+        out_shape=[jax.ShapeDtypeStruct((height, cols), jnp.float32)] * pairs,
+        compiler_params=pltpu.CompilerParams(vmem_limit_bytes=4 * MIB),
+        name="fold",
+    )(mine, got)
 
 
 def exchange(x, axis, bit):
@@ -197,8 +226,10 @@
     lens = doc_lengths.reshape(1, -1)
     docs_row = device_docs.reshape(1, -1)
     fisher = pltpu.with_memory_space_constraint(fisher_inverse, pltpu.VMEM)
-    partials = partials_call(saved_inputs, output_grads, proj_in, proj_out, lens, n_col, devices)
-    pause_call()
+    partials = partials_call(
+        saved_inputs, output_grads, proj_in, proj_out, lens, fisher_inverse, n_col, devices
+    )
+    pause_call(pause_call())
     got = lax.all_to_all(partials, ("row", "col"), 0, 0, tiled=True)
     mine = combine_call(got, lens, docs_row, tokens)
     parts = {0: mine}
@@ -212,9 +243,18 @@
     evens = [k for k in parts if k > 1]
     for k in evens:
         parts[k ^ 1] = exchange(parts[k], "col", 1)
-    sums = product_call(parts, list(range(n_col)), fisher, None, n_row)
-    shares = lax.all_to_all(sums, "row", 0, 0, tiled=True)
-    return jnp.sum(shares, axis=0)
+    (sums,) = product_call(parts, [0, 1], fisher, None, None)
+    (sums,) = product_call(parts, evens, fisher, sums, None)
+    odds = [k ^ 1 for k in evens]
+    kept, given = product_call(parts, odds, fisher, sums, n_row)
+    got = exchange(given, "row", 1)
+    shares = list(fold_call(kept, got))
+    total = shares[0]
+    for k in range(len(shares) - 1, 0, -1):
+        shares[k] = exchange(shares[k], "row", 2 * k)
+    for k in range(1, len(shares)):
+        total += shares[k]
+    return total
 
 
 def solution(mesh):

time: 66 us -> 63 us (0.955)
  waiting for transfers between devices: 19.6 us -> 15.4 us
  starting transfers between devices: 3.93 us -> 5.71 us
    all_to_all x1 -> x0, waiting for transfers between devices: 14.5 us -> none  [per_device(): shares = lax.all_to_all(sums, 'row', 0, 0, tiled=True)]
    ppermute x3 -> x7, waiting for transfers between devices: 5.08 us -> 15.4 us  [exchange(): return lax.ppermute(x, axis, [(i, i ^ bit) for i in range(size)])]
    ppermute x3 -> x7, starting transfers between devices: 0.44 us -> 5.71 us  [exchange(): return lax.ppermute(x, axis, [(i, i ^ bit) for i in range(size)])]
    all_to_all x1 -> x0, starting transfers between devices: 3.49 us -> none  [per_device(): shares = lax.all_to_all(sums, 'row', 0, 0, tiled=True)]
    reduce_sum x1 -> x0, other arithmetic: 0.72 us -> none  [per_device(): return jnp.sum(shares, axis=0)]
    add x0 -> x1, other arithmetic: none -> 0.66 us  [per_device(): total += shares[k]]
    pallas_call x1 -> x3, Pallas kernels: 3.82 us -> 3.29 us  [product_call(): pl.pallas_call(functools.partial(product_kernel, at, first is not None),...]
  transfers between devices with their start and end apart: 4 -> 7, of which waited for: 3 -> 3; matrix products, arithmetic and copies ran while one was open for 0% -> 0% of each run, Pallas kernels for 1% -> 5%
where the time goes in v4:
time: 63 us; the launch traced here: 62.9 us
  blocking collectives  19.2 us (30%)
  waiting for transfers between devices  15.4 us (24%)
  Pallas kernels  11.3 us (18%)
  local copies, waits for them, and re-layouts  10.6 us (17%)
  starting transfers between devices  5.71 us (9%)
  other arithmetic  0.66 us (1%)
    all_to_all x1, blocking collectives, per_device(): got = lax.all_to_all(partials, ('row', 'col'), 0, 0, tiled=True)  19.2 us
    ppermute x7, waiting for transfers between devices, exchange(): return lax.ppermute(x, axis, [(i, i ^ bit) for i in range(size)])  15.4 us
    unnamed x6, local copies, waits for them, and re-layouts  10.6 us
    pallas_call x1, Pallas kernels, partials_call(): pl.pallas_call(functools.partial(partials_kernel, n_col), in_specs=[pl.Bl...  6.95 us
    ppermute x7, starting transfers between devices, exchange(): return lax.ppermute(x, axis, [(i, i ^ bit) for i in range(size)])  5.71 us
    pallas_call x3, Pallas kernels, product_call(): pl.pallas_call(functools.partial(product_kernel, at, first is not None),...  3.29 us
  transfers between devices with their start and end apart: 7, of which 3 were waited for; matrix products, arithmetic and copies ran while one was open for 0% of the time, Pallas kernels for 5%

profile of v4, /device:TPU:0, one launch (start us, length us, event | category | flops | bytes accessed | tf_op | source)
XLA Modules:
  0.0 62.9 jit_solution(15001652287919222375)
XLA Ops:
  0.0 7.0 %partials.1 = f32[32,5,4,128]{3,2,1,0:T(4,128)S(1)} custom-call(s32[1,32]{1,0:T(1,128)} %bitcast.4, bf16[256,4096]{1,0:T(8,128)(2,1)} %x_in.1, bf16[256,14336]{1,0:T(8,128)(2,1)} %x_out.1, bf16[4096,128]{1,0:T(8,128)(2,1)} %w_in.1, bf16[14336,128]{1,0:T(8,128)(2,1)} %w_out.1, f32[2048,4096]{1,0:T(8,128)} %refs_1_.3), custom_call_target="tpu_custom_call" | custom-call | tf_op jit(solution)/shard_map/partials/pallas_call | solution.py:76
  7.0 19.2 %all_to_all.5 = f32[32,5,4,128]{3,2,1,0:T(4,128)S(1)} all-to-all(f32[32,5,4,128]{3,2,1,0:T(4,128)S(1)} %partials.1), channel_id=1, replica_groups=mesh['row'=8,'col'=4] {'row','col'}, dimensions={0} | all-to-all | bytes 655360 | tf_op jit(solution)/shard_map/all_to_all | solution.py:233
  26.1 0.0 copy-done.1
  26.1 0.5 combine.1.refs_0_
  26.6 0.2 collective-permute-start
  26.8 0.3 collective-permute-start.2
  27.1 3.8 %collective-permute-done.refs_0_ = f32[32,512]{1,0:T(8,128)S(1)} collective-permute-done((f32[32,512]{1,0:T(8,128)S(1)}, f32[32,512]{1,0:T(8,128)S(1)}, u32[]{:S(2)}, u32[]{:S(2)}) %collective-permute-start) | collective-permute-done | bytes 65568 | tf_op jit(solution)/shard_map/ppermute | solution.py:217
  30.9 0.0 collective-permute-start.1
  30.9 0.0 collective-permute-done.2.refs_1_
  30.9 10.5 %copy-done = f32[2048,4096]{1,0:T(8,128)S(1)} copy-done((f32[2048,4096]{1,0:T(8,128)S(1)}, f32[2048,4096]{1,0:T(8,128)}, u32[]{:S(2)}) %copy-start) | copy-done | bytes 33554456
  41.4 1.6 %shard_map.73.refs_2_ = f32[32,4096]{1,0:T(8,128)S(1)} custom-call(f32[32,512]{1,0:T(8,128)S(1)} %combine.1.refs_0_, f32[32,512]{1,0:T(8,128)S(1)} %collective-permute-done.2.refs_1_, f32[2048,4096]{1,0:T(8,128)S(1)} %copy-done), custom_call_target="tpu_custom_call" | custom-call | tf_op jit(solution)/shard_map/pallas_call | solution.py:187
  43.0 0.9 %shard_map.74.refs_2_ = f32[32,4096]{1,0:T(8,128)S(1)} custom-call(f32[32,512]{1,0:T(8,128)S(1)} %collective-permute-done.refs_0_, f32[2048,4096]{1,0:T(8,128)S(1)} %copy-done, f32[32,4096]{1,0:T(8,128)S(1)} %shard_map.73.refs_2_), custom_call_target="tpu_custom_call" | custom-call | tf_op jit(solution)/shard_map/pallas_call | solution.py:187
  43.9 0.0 collective-permute-done.1.refs_0_
  43.9 0.9 %shard_map.75 = (f32[4,4,4096]{2,1,0:T(4,128)S(1)}, f32[4,4,4096]{2,1,0:T(4,128)S(1)}) custom-call(f32[32,512]{1,0:T(8,128)S(1)} %collective-permute-done.1.refs_0_, f32[2048,4096]{1,0:T(8,128)S(1)} %copy-done, f32[32,4096]{1,0:T(8,128)S(1)} %shard_map.74.refs_2_), custom_call_target="tpu_custom_call" | custom-call | tf_op jit(solution)/shard_map/pallas_call | solution.py:187
  44.8 0.8 %collective-permute-start.3 = (f32[4,4,4096]{2,1,0:T(4,128)S(1)}, f32[4,4,4096]{2,1,0:T(4,128)S(1)}, u32[]{:S(2)}, u32[]{:S(2)}) collective-permute-start(f32[4,4,4096]{2,1,0:T(4,128)S(1)} %get-tuple-element.12), channel_id=1, source_target_pairs={{0,4},{4,0},{8,12},{12,8},{16,20},{20,16},{24,28},{28,24},{1,5},{5... | collective-permute-start | bytes 786440 | tf_op jit(solution)/shard_map/ppermute | solution.py:217
  45.6 8.0 %collective-permute-done.3.got = f32[4,4,4096]{2,1,0:T(4,128)S(1)} collective-permute-done((f32[4,4,4096]{2,1,0:T(4,128)S(1)}, f32[4,4,4096]{2,1,0:T(4,128)S(1)}, u32[]{:S(2)}, u32[]{:S(2)}) %collective-permute-start.3) | collective-permute-done | bytes 262176 | tf_op jit(solution)/shard_map/ppermute | solution.py:217
  53.6 0.9 %collective-permute-start.4 = (f32[4,4096]{1,0:T(4,128)S(1)}, f32[4,4096]{1,0:T(4,128)S(1)}, u32[]{:S(2)}, u32[]{:S(2)}) collective-permute-start(f32[4,4096]{1,0:T(4,128)S(1)} %get-tuple-element.14), channel_id=1, source_target_pairs={{0,8},{4,12},{8,0},{12,4},{16,24},{20,28},{24,16},{28,20},{1,9},{5... | collective-permute-start | bytes 196616 | tf_op jit(solution)/shard_map/ppermute | solution.py:217
  54.4 0.9 %collective-permute-start.5 = (f32[4,4096]{1,0:T(4,128)S(1)}, f32[4,4096]{1,0:T(4,128)S(1)}, u32[]{:S(2)}, u32[]{:S(2)}) collective-permute-start(f32[4,4096]{1,0:T(4,128)S(1)} %get-tuple-element.15), channel_id=1, source_target_pairs={{0,16},{4,20},{8,24},{12,28},{16,0},{20,4},{24,8},{28,12},{1,17},{... | collective-permute-start | bytes 196616 | tf_op jit(solution)/shard_map/ppermute | solution.py:217
  55.3 2.7 %collective-permute-start.6 = (f32[4,4096]{1,0:T(4,128)S(1)}, f32[4,4096]{1,0:T(4,128)S(1)}, u32[]{:S(2)}, u32[]{:S(2)}) collective-permute-start(f32[4,4096]{1,0:T(4,128)S(1)} %get-tuple-element.16), channel_id=1, source_target_pairs={{0,24},{4,28},{8,16},{12,20},{16,8},{20,12},{24,0},{28,4},{1,25},{... | collective-permute-start | bytes 196616 | tf_op jit(solution)/shard_map/ppermute | solution.py:217
  58.0 0.6 pause.3
  58.6 0.0 collective-permute-done.4
  58.6 3.6 %collective-permute-done.5 = f32[4,4096]{1,0:T(4,128)S(1)} collective-permute-done((f32[4,4096]{1,0:T(4,128)S(1)}, f32[4,4096]{1,0:T(4,128)S(1)}, u32[]{:S(2)}, u32[]{:S(2)}) %collective-permute-start.5) | collective-permute-done | bytes 65568 | tf_op jit(solution)/shard_map/ppermute | solution.py:217
  62.2 0.0 collective-permute-done.6
  62.2 0.7 %add_add_fusion = f32[4,4096]{1,0:T(4,128)} fusion(f32[4,4096]{1,0:T(4,128)S(1)} %collective-permute-done.6, f32[4,4096]{1,0:T(4,128)S(1)} %collective-permute-done.5, f32[4,4096]{1,0:T(4,128)S(1)} %get-tuple-element.13, f32[4,4096]{1,0:T(4,128)S(1)} %collective-permute-done.4), kind=kLoop, calls=%fused_computation | loop fusion | flops 49152 | bytes 327680 | tf_op jit(solution)/shard_map/add | solution.py:256
  (6 shorter events, 0.0 us)
Async XLA Ops:
  0.0 26.1 %copy-start.1 = (s32[32]{0:T(128)S(1)}, s32[32]{0:T(128)}, u32[]{:S(2)}) copy-start(s32[32]{0:T(128)} %param.11) | copy-start | bytes 388
  0.0 26.1 %copy-start.2 = (s32[32]{0:T(128)S(1)}, s32[32]{0:T(128)}, u32[]{:S(2)}) copy-start(s32[32]{0:T(128)} %param.12) | copy-start | bytes 388
  26.6 4.3 %collective-permute-start = (f32[32,512]{1,0:T(8,128)S(1)}, f32[32,512]{1,0:T(8,128)S(1)}, u32[]{:S(2)}, u32[]{:S(2)}) collective-permute-start(f32[32,512]{1,0:T(8,128)S(1)} %combine.1.refs_0_), channel_id=1, source_target_pairs={{0,2},{1,3},{2,0},{3,1},{4,6},{5,7},{6,4},{7,5},{8,10},{9,11},{10,... | collective-permute-start | bytes 196616 | tf_op jit(solution)/shard_map/ppermute | solution.py:217
  26.8 4.1 %collective-permute-start.2 = (f32[32,512]{1,0:T(8,128)S(1)}, f32[32,512]{1,0:T(8,128)S(1)}, u32[]{:S(2)}, u32[]{:S(2)}) collective-permute-start(f32[32,512]{1,0:T(8,128)S(1)} %combine.1.refs_0_), channel_id=1, source_target_pairs={{0,1},{1,0},{2,3},{3,2},{4,5},{5,4},{6,7},{7,6},{8,9},{9,8},{10,11... | collective-permute-start | bytes 196616 | tf_op jit(solution)/shard_map/ppermute | solution.py:217
  30.9 13.0 %collective-permute-start.1 = (f32[32,512]{1,0:T(8,128)S(1)}, f32[32,512]{1,0:T(8,128)S(1)}, u32[]{:S(2)}, u32[]{:S(2)}) collective-permute-start(f32[32,512]{1,0:T(8,128)S(1)} %collective-permute-done.refs_0_), channel_id=1, source_target_pairs={{0,1},{1,0},{2,3},{3,2},{4,5},{5,4},{6,7},{7,6},{8,9},{9,8},{10,11... | collective-permute-start | bytes 196616 | tf_op jit(solution)/shard_map/ppermute | solution.py:217
  30.9 10.5 %copy-start = (f32[2048,4096]{1,0:T(8,128)S(1)}, f32[2048,4096]{1,0:T(8,128)}, u32[]{:S(2)}) copy-start(f32[2048,4096]{1,0:T(8,128)} %refs_1_.3) | copy-start | bytes 100663296
  44.8 8.8 %collective-permute-start.3 = (f32[4,4,4096]{2,1,0:T(4,128)S(1)}, f32[4,4,4096]{2,1,0:T(4,128)S(1)}, u32[]{:S(2)}, u32[]{:S(2)}) collective-permute-start(f32[4,4,4096]{2,1,0:T(4,128)S(1)} %get-tuple-element.12), channel_id=1, source_target_pairs={{0,4},{4,0},{8,12},{12,8},{16,20},{20,16},{24,28},{28,24},{1,5},{5... | collective-permute-start | bytes 786440 | tf_op jit(solution)/shard_map/ppermute | solution.py:217
  53.6 5.0 %collective-permute-start.4 = (f32[4,4096]{1,0:T(4,128)S(1)}, f32[4,4096]{1,0:T(4,128)S(1)}, u32[]{:S(2)}, u32[]{:S(2)}) collective-permute-start(f32[4,4096]{1,0:T(4,128)S(1)} %get-tuple-element.14), channel_id=1, source_target_pairs={{0,8},{4,12},{8,0},{12,4},{16,24},{20,28},{24,16},{28,20},{1,9},{5... | collective-permute-start | bytes 196616 | tf_op jit(solution)/shard_map/ppermute | solution.py:217
  54.4 7.8 %collective-permute-start.5 = (f32[4,4096]{1,0:T(4,128)S(1)}, f32[4,4096]{1,0:T(4,128)S(1)}, u32[]{:S(2)}, u32[]{:S(2)}) collective-permute-start(f32[4,4096]{1,0:T(4,128)S(1)} %get-tuple-element.15), channel_id=1, source_target_pairs={{0,16},{4,20},{8,24},{12,28},{16,0},{20,4},{24,8},{28,12},{1,17},{... | collective-permute-start | bytes 196616 | tf_op jit(solution)/shard_map/ppermute | solution.py:217
  55.3 6.9 %collective-permute-start.6 = (f32[4,4096]{1,0:T(4,128)S(1)}, f32[4,4096]{1,0:T(4,128)S(1)}, u32[]{:S(2)}, u32[]{:S(2)}) collective-permute-start(f32[4,4096]{1,0:T(4,128)S(1)} %get-tuple-element.16), channel_id=1, source_target_pairs={{0,24},{4,28},{8,16},{12,20},{16,8},{20,12},{24,0},{28,4},{1,25},{... | collective-permute-start | bytes 196616 | tf_op jit(solution)/shard_map/ppermute | solution.py:217

commit v5 on v4

--- a/solution.py
+++ b/solution.py
@@ -10,6 +10,7 @@
 
 SLOTS = 5
 STEPS = 8
+HALVES = 2
 MIB = 1024 * 1024
 
 
@@ -108,7 +109,8 @@
     )(*after)
 
 
-def combine_kernel(tokens, lens, docs_row, got, out):
+def combine_kernel(tokens, lens, docs_row, mark, got, out):
+    del mark
     docs = lens.shape[1]
     pieces, rank = got.shape
     rows = out.shape[1] // rank
@@ -130,7 +132,7 @@
         )
 
 
-def combine_call(got, lens, docs_row, tokens):
+def combine_call(got, lens, docs_row, mark, tokens):
     devices, slots, rows, rank = got.shape
     docs = lens.shape[1]
     return pl.pallas_call(
@@ -138,7 +140,7 @@
         out_shape=jax.ShapeDtypeStruct((docs, rows * rank), jnp.float32),
         compiler_params=pltpu.CompilerParams(vmem_limit_bytes=4 * MIB),
         name="combine",
-    )(lens, docs_row, got.reshape(devices * slots * rows, rank))
+    )(lens, docs_row, mark, got.reshape(devices * slots * rows, rank))
 
 
 def split(x):
@@ -147,45 +149,56 @@
     return jnp.concatenate([high, low], axis=0)
 
 
-def product_kernel(at, has_first, *refs):
+def spread(values, place, mine, kept, given, where):
+    low = 1 << place
+    for at in range(len(values) // 2):
+        first = (at // low) * 2 * low + at % low
+        a, b = values[first], values[first + low]
+        kept[at, :, where] = jnp.where(mine, b, a)
+        given[at, :, where] = jnp.where(mine, a, b)
+
+
+def has_bit(bit):
+    return lax.rem(lax.div(lax.axis_index("row"), bit), 2) == 1
+
+
+def product_kernel(at, has_first, half, bit, *refs):
     parts, refs = refs[: len(at)], refs[len(at) :]
     f_ref, outs = refs[0], refs[1 + has_first :]
     docs, size = parts[0].shape
-    cols = f_ref.shape[1]
+    cols = outs[0].shape[-1]
+    base = 0 if half is None else half * cols
     me = lax.axis_index("col")
     both = [split(part[...]) for part in parts]
     width = 512 if cols % 512 == 0 else cols
     for n in range(cols // width):
         where = slice(n * width, (n + 1) * width)
+        source = slice(base + n * width, base + (n + 1) * width)
         total = jnp.zeros((2 * docs, width), jnp.float32)
         for k, x in zip(at, both):
             rows = pl.ds(pl.multiple_of(jnp.bitwise_xor(me, k) * size, size), size)
-            tile = f_ref[rows, where].astype(jnp.bfloat16)
+            tile = f_ref[rows, source].astype(jnp.bfloat16)
             total += jnp.dot(x, tile, preferred_element_type=jnp.float32)
         total = total[:docs] + total[docs:]
         if has_first:
-            total += refs[1][:, where]
-        if len(outs) == 1:
+            total += refs[1][:, source]
+        if half is None:
             outs[0][:, where] = total
             continue
         groups, height, _ = outs[0].shape
-        second = lax.rem(lax.axis_index("row"), 2) == 1
-        for g in range(groups):
-            a = total[2 * g * height : (2 * g + 1) * height]
-            b = total[(2 * g + 1) * height : (2 * g + 2) * height]
-            outs[0][g, :, where] = jnp.where(second, b, a)
-            outs[1][g, :, where] = jnp.where(second, a, b)
-
-
-def product_call(parts, at, fisher, first, groups):
+        values = [total[g * height : (g + 1) * height] for g in range(2 * groups)]
+        spread(values, bit.bit_length() - 1, has_bit(bit), *outs, where)
+
+
+def product_call(parts, at, fisher, first, groups=None, half=None, bit=None):
     docs = parts[at[0]].shape[0]
     cols = fisher.shape[1]
     shape, count = (docs, cols), 1
-    if groups is not None:
-        shape, count = (groups // 2, docs // groups, cols), 2
+    if half is not None:
+        shape, count = (groups // 2, docs // groups, cols // HALVES), 2
     args = [parts[k] for k in at] + [fisher] + ([] if first is None else [first])
     return pl.pallas_call(
-        functools.partial(product_kernel, at, first is not None),
+        functools.partial(product_kernel, at, first is not None, half, bit),
         in_specs=[pl.BlockSpec(memory_space=pltpu.VMEM)] * len(args),
         out_specs=[pl.BlockSpec(memory_space=pltpu.VMEM)] * count,
         out_shape=[jax.ShapeDtypeStruct(shape, jnp.float32)] * count,
@@ -193,23 +206,45 @@
     )(*args)
 
 
-def fold_kernel(mine, got, *outs):
-    me = lax.div(lax.axis_index("row"), 2)
-    for k, out in enumerate(outs):
-        at = jnp.bitwise_xor(me, k)
-        out[...] = mine[at] + got[at]
-
-
-def fold_call(mine, got):
-    pairs, height, cols = mine.shape
-    return pl.pallas_call(
-        fold_kernel,
+def fold_kernel(place, bit, mine, got, kept, given):
+    values = [mine[g] + got[g] for g in range(mine.shape[0])]
+    spread(values, place, has_bit(bit), kept, given, slice(None))
+
+
+def fold_call(mine, got, place, bit):
+    groups, height, cols = mine.shape
+    return pl.pallas_call(
+        functools.partial(fold_kernel, place, bit),
         in_specs=[pl.BlockSpec(memory_space=pltpu.VMEM)] * 2,
-        out_specs=[pl.BlockSpec(memory_space=pltpu.VMEM)] * pairs,
-        out_shape=[jax.ShapeDtypeStruct((height, cols), jnp.float32)] * pairs,
+        out_specs=[pl.BlockSpec(memory_space=pltpu.VMEM)] * 2,
+        out_shape=[jax.ShapeDtypeStruct((groups // 2, height, cols), jnp.float32)] * 2,
         compiler_params=pltpu.CompilerParams(vmem_limit_bytes=4 * MIB),
-        name="fold",
     )(mine, got)
+
+
+def finish_kernel(*refs):
+    pieces, out = refs[:-1], refs[-1]
+    cols = pieces[0].shape[-1]
+    for half in range(len(pieces) // 2):
+        where = slice(half * cols, (half + 1) * cols)
+        out[:, where] = pieces[2 * half][0] + pieces[2 * half + 1][0]
+
+
+def finish_call(pieces):
+    _, height, cols = pieces[0].shape
+    return pl.pallas_call(
+        finish_kernel,
+        in_specs=[pl.BlockSpec(memory_space=pltpu.VMEM)] * len(pieces),
+        out_specs=pl.BlockSpec(memory_space=pltpu.VMEM),
+        out_shape=jax.ShapeDtypeStruct((height, len(pieces) // 2 * cols), jnp.float32),
+        compiler_params=pltpu.CompilerParams(vmem_limit_bytes=4 * MIB),
+        name="finish",
+    )(*pieces)
+
+
+def bit_orders(n_row):
+    bits = [1 << p for p in range(n_row.bit_length() - 1)]
+    return bits, [bits[1], bits[0]] + bits[2:]
 
 
 def exchange(x, axis, bit):
@@ -229,9 +264,9 @@
     partials = partials_call(
         saved_inputs, output_grads, proj_in, proj_out, lens, fisher_inverse, n_col, devices
     )
-    pause_call(pause_call())
+    mark = pause_call(pause_call())
     got = lax.all_to_all(partials, ("row", "col"), 0, 0, tiled=True)
-    mine = combine_call(got, lens, docs_row, tokens)
+    mine = combine_call(got, lens, docs_row, mark, tokens)
     parts = {0: mine}
     bit = n_col // 2
     parts[bit] = exchange(mine, "col", bit)
@@ -243,18 +278,27 @@
     evens = [k for k in parts if k > 1]
     for k in evens:
         parts[k ^ 1] = exchange(parts[k], "col", 1)
-    (sums,) = product_call(parts, [0, 1], fisher, None, None)
-    (sums,) = product_call(parts, evens, fisher, sums, None)
+    (sums,) = product_call(parts, [0, 1], fisher, None)
+    (sums,) = product_call(parts, evens, fisher, sums)
     odds = [k ^ 1 for k in evens]
-    kept, given = product_call(parts, odds, fisher, sums, n_row)
-    got = exchange(given, "row", 1)
-    shares = list(fold_call(kept, got))
-    total = shares[0]
-    for k in range(len(shares) - 1, 0, -1):
-        shares[k] = exchange(shares[k], "row", 2 * k)
-    for k in range(1, len(shares)):
-        total += shares[k]
-    return total
+    orders = bit_orders(n_row)
+    held, left = [], []
+    for half, bits in enumerate(orders):
+        held.append(product_call(parts, odds, fisher, sums, n_row, half, bits[0]))
+        left.append(sorted(set(bits) - {bits[0]}))
+    pieces = []
+    for stage in range(len(orders[0])):
+        for half, bits in enumerate(orders):
+            kept, given = held[half]
+            got = exchange(given, "row", bits[stage])
+            if not left[half]:
+                pieces += [kept, got]
+                continue
+            bit = bits[stage + 1]
+            place = left[half].index(bit)
+            left[half].remove(bit)
+            held[half] = fold_call(kept, got, place, bit)
+    return finish_call(pieces)
 
 
 def solution(mesh):

time: 63 us -> 62.4 us (level)
  blocking collectives: 19.2 us -> 0 us
  waiting for transfers between devices: 15.4 us -> 25.3 us
  starting transfers between devices: 5.71 us -> 14 us
  Pallas kernels: 11.3 us -> 12.2 us
  other arithmetic: 0.66 us -> 0 us
    all_to_all x1 -> x0, blocking collectives: 19.2 us -> none  [per_device(): got = lax.all_to_all(partials, ('row', 'col'), 0, 0, tiled=True)]
    all_to_all x0 -> x1, waiting for transfers between devices: none -> 12 us  [per_device(): got = lax.all_to_all(partials, ('row', 'col'), 0, 0, tiled=True)]
    all_to_all x0 -> x1, starting transfers between devices: none -> 7.33 us  [per_device(): got = lax.all_to_all(partials, ('row', 'col'), 0, 0, tiled=True)]
    ppermute x7 -> x9, waiting for transfers between devices: 15.4 us -> 13.3 us  [exchange(): return lax.ppermute(x, axis, [(i, i ^ bit) for i in range(size)])]
    ppermute x7 -> x9, starting transfers between devices: 5.71 us -> 6.71 us  [exchange(): return lax.ppermute(x, axis, [(i, i ^ bit) for i in range(size)])]
    pallas_call x4 -> x9, Pallas kernels: 3.32 us -> 4.11 us  [the longest x4 3.4 us: product_call(): pl.pallas_call(functools.partial(product_kernel, at, first is not None, h...]
    add x1 -> x0, other arithmetic: 0.66 us -> none  [per_device(): total += shares[k]]
    pallas_call x1, Pallas kernels: 6.95 us -> 7.61 us  [partials_call(): pl.pallas_call(functools.partial(partials_kernel, n_col), in_specs=[pl.Bl...]
  transfers between devices with their start and end apart: 7 -> 10, of which waited for: 3 -> 8; matrix products, arithmetic and copies ran while one was open for 0% -> 0% of each run, Pallas kernels for 5% -> 5%
where the time goes in v5:
time: 62.4 us; the launch traced here: 62.2 us
  waiting for transfers between devices  25.3 us (41%)
  starting transfers between devices  14 us (22%)
  Pallas kernels  12.2 us (20%)
  local copies, waits for them, and re-layouts  10.6 us (17%)
    ppermute x9, waiting for transfers between devices, exchange(): return lax.ppermute(x, axis, [(i, i ^ bit) for i in range(size)])  13.3 us
    all_to_all x1, waiting for transfers between devices, per_device(): got = lax.all_to_all(partials, ('row', 'col'), 0, 0, tiled=True)  12 us
    unnamed x6, local copies, waits for them, and re-layouts  10.6 us
    pallas_call x1, Pallas kernels, partials_call(): pl.pallas_call(functools.partial(partials_kernel, n_col), in_specs=[pl.Bl...  7.61 us
    all_to_all x1, starting transfers between devices, per_device(): got = lax.all_to_all(partials, ('row', 'col'), 0, 0, tiled=True)  7.33 us
    ppermute x9, starting transfers between devices, exchange(): return lax.ppermute(x, axis, [(i, i ^ bit) for i in range(size)])  6.71 us
    pallas_call x4, Pallas kernels, product_call(): pl.pallas_call(functools.partial(product_kernel, at, first is not None, h...  3.4 us
  transfers between devices with their start and end apart: 10, of which 8 were waited for; matrix products, arithmetic and copies ran while one was open for 0% of the time, Pallas kernels for 5%

profile of v5, /device:TPU:0, one launch (start us, length us, event | category | flops | bytes accessed | tf_op | source)
XLA Modules:
  0.0 62.2 jit_solution(11980796813447298371)
XLA Ops:
  0.0 7.6 %partials.1 = f32[32,5,4,128]{3,2,1,0:T(4,128)} custom-call(s32[1,32]{1,0:T(1,128)} %bitcast.4, bf16[256,4096]{1,0:T(8,128)(2,1)} %x_in.1, bf16[256,14336]{1,0:T(8,128)(2,1)} %x_out.1, bf16[4096,128]{1,0:T(8,128)(2,1)} %w_in.1, bf16[14336,128]{1,0:T(8,128)(2,1)} %w_out.1, f32[2048,4096]{1,0:T(8,128)} %refs_1_.5), custom_call_target="tpu_custom_call" | custom-call | tf_op jit(solution)/shard_map/partials/pallas_call | solution.py:77
  7.6 7.3 %all-to-all-start = ((f32[32,5,4,128]{3,2,1,0:T(4,128)}), f32[32,5,4,128]{3,2,1,0:T(4,128)S(1)}, u32[]{:S(2)}, u32[]{:S(2)}) async-start(f32[32,5,4,128]{3,2,1,0:T(4,128)} %partials.1), calls=%async_computation | async-start | bytes 655360 | tf_op jit(solution)/shard_map/all_to_all | solution.py:268
  15.0 12.0 %all-to-all-done = f32[32,5,4,128]{3,2,1,0:T(4,128)S(1)} async-done(((f32[32,5,4,128]{3,2,1,0:T(4,128)}), f32[32,5,4,128]{3,2,1,0:T(4,128)S(1)}, u32[]{:S(2)}, u32[]{:S(2)}) %all-to-all-start) | async-done | bytes 327712 | tf_op jit(solution)/shard_map/all_to_all | solution.py:268
  27.0 0.5 combine.1.refs_0_
  27.7 0.3 collective-permute-start.2
  27.9 3.8 %collective-permute-done.refs_0_ = f32[32,512]{1,0:T(8,128)S(1)} collective-permute-done((f32[32,512]{1,0:T(8,128)S(1)}, f32[32,512]{1,0:T(8,128)S(1)}, u32[]{:S(2)}, u32[]{:S(2)}) %collective-permute-start) | collective-permute-done | bytes 65568 | tf_op jit(solution)/shard_map/ppermute | solution.py:252
  31.8 10.5 %copy-done = f32[2048,4096]{1,0:T(8,128)S(1)} copy-done((f32[2048,4096]{1,0:T(8,128)S(1)}, f32[2048,4096]{1,0:T(8,128)}, u32[]{:S(2)}) %copy-start) | copy-done | bytes 33554456
  42.3 1.6 %shard_map.73.refs_2_ = f32[32,4096]{1,0:T(8,128)S(1)} custom-call(f32[32,512]{1,0:T(8,128)S(1)} %combine.1.refs_0_, f32[32,512]{1,0:T(8,128)S(1)} %collective-permute-done.2.refs_1_, f32[2048,4096]{1,0:T(8,128)S(1)} %copy-done), custom_call_target="tpu_custom_call" | custom-call | tf_op jit(solution)/shard_map/pallas_call | solution.py:200
  43.9 0.9 %shard_map.74.refs_2_ = f32[32,4096]{1,0:T(8,128)S(1)} custom-call(f32[32,512]{1,0:T(8,128)S(1)} %collective-permute-done.refs_0_, f32[2048,4096]{1,0:T(8,128)S(1)} %copy-done, f32[32,4096]{1,0:T(8,128)S(1)} %shard_map.73.refs_2_), custom_call_target="tpu_custom_call" | custom-call | tf_op jit(solution)/shard_map/pallas_call | solution.py:200
  44.7 0.5 shard_map.78
  45.2 0.8 %collective-permute-start.6 = (f32[4,4,2048]{2,1,0:T(4,128)S(1)}, f32[4,4,2048]{2,1,0:T(4,128)S(1)}, u32[]{:S(2)}, u32[]{:S(2)}) collective-permute-start(f32[4,4,2048]{2,1,0:T(4,128)S(1)} %get-tuple-element.24), channel_id=1, source_target_pairs={{0,8},{4,12},{8,0},{12,4},{16,24},{20,28},{24,16},{28,20},{1,9},{5... | collective-permute-start | bytes 393224 | tf_op jit(solution)/shard_map/ppermute | solution.py:252
  46.1 0.5 shard_map.75
  46.6 0.7 %collective-permute-start.3 = (f32[4,4,2048]{2,1,0:T(4,128)S(1)}, f32[4,4,2048]{2,1,0:T(4,128)S(1)}, u32[]{:S(2)}, u32[]{:S(2)}) collective-permute-start(f32[4,4,2048]{2,1,0:T(4,128)S(1)} %get-tuple-element.18), channel_id=1, source_target_pairs={{0,4},{4,0},{8,12},{12,8},{16,20},{20,16},{24,28},{28,24},{1,5},{5... | collective-permute-start | bytes 393224 | tf_op jit(solution)/shard_map/ppermute | solution.py:252
  47.3 3.9 %collective-permute-done.6.got = f32[4,4,2048]{2,1,0:T(4,128)S(1)} collective-permute-done((f32[4,4,2048]{2,1,0:T(4,128)S(1)}, f32[4,4,2048]{2,1,0:T(4,128)S(1)}, u32[]{:S(2)}, u32[]{:S(2)}) %collective-permute-start.6) | collective-permute-done | bytes 131104 | tf_op jit(solution)/shard_map/ppermute | solution.py:252
  51.2 0.8 %collective-permute-start.7 = (f32[2,4,2048]{2,1,0:T(4,128)S(1)}, f32[2,4,2048]{2,1,0:T(4,128)S(1)}, u32[]{:S(2)}, u32[]{:S(2)}) collective-permute-start(f32[2,4,2048]{2,1,0:T(4,128)S(1)} %get-tuple-element.26), channel_id=1, source_target_pairs={{0,4},{4,0},{8,12},{12,8},{16,20},{20,16},{24,28},{28,24},{1,5},{5... | collective-permute-start | bytes 196616 | tf_op jit(solution)/shard_map/ppermute | solution.py:252
  52.1 0.2 collective-permute-done.3.got
  52.3 1.3 %collective-permute-start.4 = (f32[2,4,2048]{2,1,0:T(4,128)S(1)}, f32[2,4,2048]{2,1,0:T(4,128)S(1)}, u32[]{:S(2)}, u32[]{:S(2)}) collective-permute-start(f32[2,4,2048]{2,1,0:T(4,128)S(1)} %get-tuple-element.20), channel_id=1, source_target_pairs={{0,8},{4,12},{8,0},{12,4},{16,24},{20,28},{24,16},{28,20},{1,9},{5... | collective-permute-start | bytes 196616 | tf_op jit(solution)/shard_map/ppermute | solution.py:252
  53.6 1.9 %collective-permute-done.7.got = f32[2,4,2048]{2,1,0:T(4,128)S(1)} collective-permute-done((f32[2,4,2048]{2,1,0:T(4,128)S(1)}, f32[2,4,2048]{2,1,0:T(4,128)S(1)}, u32[]{:S(2)}, u32[]{:S(2)}) %collective-permute-start.7) | collective-permute-done | bytes 65568 | tf_op jit(solution)/shard_map/ppermute | solution.py:252
  55.6 0.6 collective-permute-start.8
  56.2 0.5 collective-permute-done.4.got
  56.7 2.0 %collective-permute-start.5 = (f32[1,4,2048]{2,1,0:T(4,128)S(1)}, f32[1,4,2048]{2,1,0:T(4,128)S(1)}, u32[]{:S(2)}, u32[]{:S(2)}) collective-permute-start(f32[1,4,2048]{2,1,0:T(4,128)S(1)} %get-tuple-element.22), channel_id=1, source_target_pairs={{0,16},{4,20},{8,24},{12,28},{16,0},{20,4},{24,8},{28,12},{1,17},{... | collective-permute-start | bytes 98312 | tf_op jit(solution)/shard_map/ppermute | solution.py:252
  58.7 2.1 %collective-permute-done.8.refs_3_ = f32[1,4,2048]{2,1,0:T(4,128)S(1)} collective-permute-done((f32[1,4,2048]{2,1,0:T(4,128)S(1)}, f32[1,4,2048]{2,1,0:T(4,128)S(1)}, u32[]{:S(2)}, u32[]{:S(2)}) %collective-permute-start.8) | collective-permute-done | bytes 32800 | tf_op jit(solution)/shard_map/ppermute | solution.py:252
  60.8 0.7 %collective-permute-done.5.refs_1_ = f32[1,4,2048]{2,1,0:T(4,128)S(1)} collective-permute-done((f32[1,4,2048]{2,1,0:T(4,128)S(1)}, f32[1,4,2048]{2,1,0:T(4,128)S(1)}, u32[]{:S(2)}, u32[]{:S(2)}) %collective-permute-start.5) | collective-permute-done | bytes 32800 | tf_op jit(solution)/shard_map/ppermute | solution.py:252
  61.5 0.6 %finish.1 = f32[4,4096]{1,0:T(4,128)} custom-call(f32[1,4,2048]{2,1,0:T(4,128)S(1)} %get-tuple-element.21.refs_0_, f32[1,4,2048]{2,1,0:T(4,128)S(1)} %collective-permute-done.5.refs_1_, f32[1,4,2048]{2,1,0:T(4,128)S(1)} %get-tuple-element.27.refs_2_, f32[1,4,2048]{2,1,0:T(4,128)S(1)} %collective-permute-done.8.refs_3_), custom_call_target="tpu_custom_call" | custom-call | tf_op jit(solution)/shard_map/finish/pallas_call | solution.py:235
  (15 shorter events, 0.3 us)
Async XLA Ops:
  7.6 19.4 %all-to-all-start = ((f32[32,5,4,128]{3,2,1,0:T(4,128)}), f32[32,5,4,128]{3,2,1,0:T(4,128)S(1)}, u32[]{:S(2)}, u32[]{:S(2)}) async-start(f32[32,5,4,128]{3,2,1,0:T(4,128)} %partials.1), calls=%async_computation | async-start | bytes 655360 | tf_op jit(solution)/shard_map/all_to_all | solution.py:268
  15.0 12.0 %copy-start.1 = (s32[32]{0:T(128)S(1)}, s32[32]{0:T(128)}, u32[]{:S(2)}) copy-start(s32[32]{0:T(128)} %param.11) | copy-start | bytes 388
  15.0 12.0 %copy-start.2 = (s32[32]{0:T(128)S(1)}, s32[32]{0:T(128)}, u32[]{:S(2)}) copy-start(s32[32]{0:T(128)} %param.12) | copy-start | bytes 388
  27.5 4.3 %collective-permute-start = (f32[32,512]{1,0:T(8,128)S(1)}, f32[32,512]{1,0:T(8,128)S(1)}, u32[]{:S(2)}, u32[]{:S(2)}) collective-permute-start(f32[32,512]{1,0:T(8,128)S(1)} %combine.1.refs_0_), channel_id=1, source_target_pairs={{0,2},{1,3},{2,0},{3,1},{4,6},{5,7},{6,4},{7,5},{8,10},{9,11},{10,... | collective-permute-start | bytes 196616 | tf_op jit(solution)/shard_map/ppermute | solution.py:252
  27.7 4.1 %collective-permute-start.2 = (f32[32,512]{1,0:T(8,128)S(1)}, f32[32,512]{1,0:T(8,128)S(1)}, u32[]{:S(2)}, u32[]{:S(2)}) collective-permute-start(f32[32,512]{1,0:T(8,128)S(1)} %combine.1.refs_0_), channel_id=1, source_target_pairs={{0,1},{1,0},{2,3},{3,2},{4,5},{5,4},{6,7},{7,6},{8,9},{9,8},{10,11... | collective-permute-start | bytes 196616 | tf_op jit(solution)/shard_map/ppermute | solution.py:252
  31.7 13.0 %collective-permute-start.1 = (f32[32,512]{1,0:T(8,128)S(1)}, f32[32,512]{1,0:T(8,128)S(1)}, u32[]{:S(2)}, u32[]{:S(2)}) collective-permute-start(f32[32,512]{1,0:T(8,128)S(1)} %collective-permute-done.refs_0_), channel_id=1, source_target_pairs={{0,1},{1,0},{2,3},{3,2},{4,5},{5,4},{6,7},{7,6},{8,9},{9,8},{10,11... | collective-permute-start | bytes 196616 | tf_op jit(solution)/shard_map/ppermute | solution.py:252
  31.8 10.5 %copy-start = (f32[2048,4096]{1,0:T(8,128)S(1)}, f32[2048,4096]{1,0:T(8,128)}, u32[]{:S(2)}) copy-start(f32[2048,4096]{1,0:T(8,128)} %refs_1_.5) | copy-start | bytes 100663296
  45.2 6.0 %collective-permute-start.6 = (f32[4,4,2048]{2,1,0:T(4,128)S(1)}, f32[4,4,2048]{2,1,0:T(4,128)S(1)}, u32[]{:S(2)}, u32[]{:S(2)}) collective-permute-start(f32[4,4,2048]{2,1,0:T(4,128)S(1)} %get-tuple-element.24), channel_id=1, source_target_pairs={{0,8},{4,12},{8,0},{12,4},{16,24},{20,28},{24,16},{28,20},{1,9},{5... | collective-permute-start | bytes 393224 | tf_op jit(solution)/shard_map/ppermute | solution.py:252
  46.6 5.7 %collective-permute-start.3 = (f32[4,4,2048]{2,1,0:T(4,128)S(1)}, f32[4,4,2048]{2,1,0:T(4,128)S(1)}, u32[]{:S(2)}, u32[]{:S(2)}) collective-permute-start(f32[4,4,2048]{2,1,0:T(4,128)S(1)} %get-tuple-element.18), channel_id=1, source_target_pairs={{0,4},{4,0},{8,12},{12,8},{16,20},{20,16},{24,28},{28,24},{1,5},{5... | collective-permute-start | bytes 393224 | tf_op jit(solution)/shard_map/ppermute | solution.py:252
  51.2 4.3 %collective-permute-start.7 = (f32[2,4,2048]{2,1,0:T(4,128)S(1)}, f32[2,4,2048]{2,1,0:T(4,128)S(1)}, u32[]{:S(2)}, u32[]{:S(2)}) collective-permute-start(f32[2,4,2048]{2,1,0:T(4,128)S(1)} %get-tuple-element.26), channel_id=1, source_target_pairs={{0,4},{4,0},{8,12},{12,8},{16,20},{20,16},{24,28},{28,24},{1,5},{5... | collective-permute-start | bytes 196616 | tf_op jit(solution)/shard_map/ppermute | solution.py:252
  52.3 4.3 %collective-permute-start.4 = (f32[2,4,2048]{2,1,0:T(4,128)S(1)}, f32[2,4,2048]{2,1,0:T(4,128)S(1)}, u32[]{:S(2)}, u32[]{:S(2)}) collective-permute-start(f32[2,4,2048]{2,1,0:T(4,128)S(1)} %get-tuple-element.20), channel_id=1, source_target_pairs={{0,8},{4,12},{8,0},{12,4},{16,24},{20,28},{24,16},{28,20},{1,9},{5... | collective-permute-start | bytes 196616 | tf_op jit(solution)/shard_map/ppermute | solution.py:252
  55.6 5.2 %collective-permute-start.8 = (f32[1,4,2048]{2,1,0:T(4,128)S(1)}, f32[1,4,2048]{2,1,0:T(4,128)S(1)}, u32[]{:S(2)}, u32[]{:S(2)}) collective-permute-start(f32[1,4,2048]{2,1,0:T(4,128)S(1)} %get-tuple-element.28), channel_id=1, source_target_pairs={{0,16},{4,20},{8,24},{12,28},{16,0},{20,4},{24,8},{28,12},{1,17},{... | collective-permute-start | bytes 98312 | tf_op jit(solution)/shard_map/ppermute | solution.py:252
  56.7 4.9 %collective-permute-start.5 = (f32[1,4,2048]{2,1,0:T(4,128)S(1)}, f32[1,4,2048]{2,1,0:T(4,128)S(1)}, u32[]{:S(2)}, u32[]{:S(2)}) collective-permute-start(f32[1,4,2048]{2,1,0:T(4,128)S(1)} %get-tuple-element.22), channel_id=1, source_target_pairs={{0,16},{4,20},{8,24},{12,28},{16,0},{20,4},{24,8},{28,12},{1,17},{... | collective-permute-start | bytes 98312 | tf_op jit(solution)/shard_map/ppermute | solution.py:252

commit v6 on v4

--- a/solution.py
+++ b/solution.py
@@ -10,6 +10,8 @@
 
 SLOTS = 5
 STEPS = 8
+QUAD = 4
+TURNS = (1, 2, 3)
 MIB = 1024 * 1024
 
 
@@ -108,7 +110,8 @@
     )(*after)
 
 
-def combine_kernel(tokens, lens, docs_row, got, out):
+def combine_kernel(tokens, lens, docs_row, mark, got, out):
+    del mark
     docs = lens.shape[1]
     pieces, rank = got.shape
     rows = out.shape[1] // rank
@@ -130,7 +133,7 @@
         )
 
 
-def combine_call(got, lens, docs_row, tokens):
+def combine_call(got, lens, docs_row, mark, tokens):
     devices, slots, rows, rank = got.shape
     docs = lens.shape[1]
     return pl.pallas_call(
@@ -138,7 +141,7 @@
         out_shape=jax.ShapeDtypeStruct((docs, rows * rank), jnp.float32),
         compiler_params=pltpu.CompilerParams(vmem_limit_bytes=4 * MIB),
         name="combine",
-    )(lens, docs_row, got.reshape(devices * slots * rows, rank))
+    )(lens, docs_row, mark, got.reshape(devices * slots * rows, rank))
 
 
 def split(x):
@@ -168,48 +171,71 @@
         if len(outs) == 1:
             outs[0][:, where] = total
             continue
-        groups, height, _ = outs[0].shape
-        second = lax.rem(lax.axis_index("row"), 2) == 1
+        groups, height, _ = outs[-1].shape
         for g in range(groups):
-            a = total[2 * g * height : (2 * g + 1) * height]
-            b = total[(2 * g + 1) * height : (2 * g + 2) * height]
-            outs[0][g, :, where] = jnp.where(second, b, a)
-            outs[1][g, :, where] = jnp.where(second, a, b)
-
-
-def product_call(parts, at, fisher, first, groups):
+            outs[-1][g, :, where] = total[g * height : (g + 1) * height]
+    if len(outs) > 1:
+        cross, own, held = outs[:QUAD], outs[QUAD:-1], outs[-1]
+        row = lax.axis_index("row")
+        for k in range(QUAD):
+            own[k][...] = held[jnp.bitwise_xor(row, k)]
+            for t in range(1, held.shape[0] // QUAD):
+                cross[k][t - 1] = held[jnp.bitwise_xor(row, QUAD * t + k)]
+
+
+def product_call(parts, at, fisher, first, groups=None):
     docs = parts[at[0]].shape[0]
     cols = fisher.shape[1]
-    shape, count = (docs, cols), 1
+    shapes, scratch = [(docs, cols)], []
     if groups is not None:
-        shape, count = (groups // 2, docs // groups, cols), 2
+        height = docs // groups
+        shapes = [(groups // QUAD - 1, height, cols)] * QUAD + [(height, cols)] * QUAD
+        scratch = [pltpu.VMEM((groups, height, cols), jnp.float32)]
     args = [parts[k] for k in at] + [fisher] + ([] if first is None else [first])
     return pl.pallas_call(
         functools.partial(product_kernel, at, first is not None),
         in_specs=[pl.BlockSpec(memory_space=pltpu.VMEM)] * len(args),
-        out_specs=[pl.BlockSpec(memory_space=pltpu.VMEM)] * count,
-        out_shape=[jax.ShapeDtypeStruct(shape, jnp.float32)] * count,
+        out_specs=[pl.BlockSpec(memory_space=pltpu.VMEM)] * len(shapes),
+        out_shape=[jax.ShapeDtypeStruct(shape, jnp.float32) for shape in shapes],
+        scratch_shapes=scratch,
         compiler_params=pltpu.CompilerParams(vmem_limit_bytes=12 * MIB),
     )(*args)
 
 
-def fold_kernel(mine, got, *outs):
-    me = lax.div(lax.axis_index("row"), 2)
-    for k, out in enumerate(outs):
-        at = jnp.bitwise_xor(me, k)
-        out[...] = mine[at] + got[at]
-
-
-def fold_call(mine, got):
-    pairs, height, cols = mine.shape
+def fold_kernel(*refs):
+    pieces, outs = refs[:QUAD], refs[QUAD:]
+    for t, out in enumerate(outs):
+        out[...] = (pieces[0][t] + pieces[1][t]) + (pieces[2][t] + pieces[3][t])
+
+
+def fold_call(pieces):
+    others, height, cols = pieces[0].shape
     return pl.pallas_call(
         fold_kernel,
-        in_specs=[pl.BlockSpec(memory_space=pltpu.VMEM)] * 2,
-        out_specs=[pl.BlockSpec(memory_space=pltpu.VMEM)] * pairs,
-        out_shape=[jax.ShapeDtypeStruct((height, cols), jnp.float32)] * pairs,
+        in_specs=[pl.BlockSpec(memory_space=pltpu.VMEM)] * QUAD,
+        out_specs=[pl.BlockSpec(memory_space=pltpu.VMEM)] * others,
+        out_shape=[jax.ShapeDtypeStruct((height, cols), jnp.float32)] * others,
         compiler_params=pltpu.CompilerParams(vmem_limit_bytes=4 * MIB),
         name="fold",
-    )(mine, got)
+    )(*pieces)
+
+
+def finish_kernel(*refs):
+    total = refs[0][...]
+    for piece in refs[1:-1]:
+        total += piece[...]
+    refs[-1][...] = total
+
+
+def finish_call(pieces):
+    return pl.pallas_call(
+        finish_kernel,
+        in_specs=[pl.BlockSpec(memory_space=pltpu.VMEM)] * len(pieces),
+        out_specs=pl.BlockSpec(memory_space=pltpu.VMEM),
+        out_shape=jax.ShapeDtypeStruct(pieces[0].shape, jnp.float32),
+        compiler_params=pltpu.CompilerParams(vmem_limit_bytes=4 * MIB),
+        name="finish",
+    )(*pieces)
 
 
 def exchange(x, axis, bit):
@@ -229,9 +255,9 @@
     partials = partials_call(
         saved_inputs, output_grads, proj_in, proj_out, lens, fisher_inverse, n_col, devices
     )
-    pause_call(pause_call())
+    mark = pause_call(pause_call())
     got = lax.all_to_all(partials, ("row", "col"), 0, 0, tiled=True)
-    mine = combine_call(got, lens, docs_row, tokens)
+    mine = combine_call(got, lens, docs_row, mark, tokens)
     parts = {0: mine}
     bit = n_col // 2
     parts[bit] = exchange(mine, "col", bit)
@@ -243,18 +269,19 @@
     evens = [k for k in parts if k > 1]
     for k in evens:
         parts[k ^ 1] = exchange(parts[k], "col", 1)
-    (sums,) = product_call(parts, [0, 1], fisher, None, None)
-    (sums,) = product_call(parts, evens, fisher, sums, None)
+    (sums,) = product_call(parts, [0, 1], fisher, None)
+    (sums,) = product_call(parts, evens, fisher, sums)
     odds = [k ^ 1 for k in evens]
-    kept, given = product_call(parts, odds, fisher, sums, n_row)
-    got = exchange(given, "row", 1)
-    shares = list(fold_call(kept, got))
-    total = shares[0]
-    for k in range(len(shares) - 1, 0, -1):
-        shares[k] = exchange(shares[k], "row", 2 * k)
-    for k in range(1, len(shares)):
-        total += shares[k]
-    return total
+    results = product_call(parts, odds, fisher, sums, n_row)
+    cross, own = list(results[:QUAD]), list(results[QUAD:])
+    for k in TURNS:
+        cross[k] = exchange(cross[k], "row", k)
+    for k in TURNS:
+        own[k] = exchange(own[k], "row", k)
+    far = fold_call(cross)
+    for t, piece in enumerate(far):
+        own.append(exchange(piece, "row", QUAD * (t + 1)))
+    return finish_call(own)
 
 
 def solution(mesh):

time: 63 us -> 59.8 us (0.949)
  blocking collectives: 19.2 us -> 0 us
  starting transfers between devices: 5.71 us -> 15.5 us
  waiting for transfers between devices: 15.4 us -> 21.3 us
  Pallas kernels: 11.3 us -> 12 us
  other arithmetic: 0.66 us -> 0 us
    all_to_all x1 -> x0, blocking collectives: 19.2 us -> none  [per_device(): got = lax.all_to_all(partials, ('row', 'col'), 0, 0, tiled=True)]
    all_to_all x0 -> x1, waiting for transfers between devices: none -> 12 us  [per_device(): got = lax.all_to_all(partials, ('row', 'col'), 0, 0, tiled=True)]
    all_to_all x0 -> x1, starting transfers between devices: none -> 7.33 us  [per_device(): got = lax.all_to_all(partials, ('row', 'col'), 0, 0, tiled=True)]
    ppermute x7 -> x10, waiting for transfers between devices: 15.4 us -> 9.32 us  [exchange(): return lax.ppermute(x, axis, [(i, i ^ bit) for i in range(size)])]
    ppermute x7 -> x10, starting transfers between devices: 5.71 us -> 8.21 us  [exchange(): return lax.ppermute(x, axis, [(i, i ^ bit) for i in range(size)])]
    add x1 -> x0, other arithmetic: 0.66 us -> none  [per_device(): total += shares[k]]
    pallas_call x0 -> x1, Pallas kernels: none -> 0.65 us  [finish_call(): pl.pallas_call(finish_kernel, in_specs=[pl.BlockSpec(memory_space=pltpu.V...]
    pallas_call x1, Pallas kernels: 6.95 us -> 7.6 us  [partials_call(): pl.pallas_call(functools.partial(partials_kernel, n_col), in_specs=[pl.Bl...]
  transfers between devices with their start and end apart: 7 -> 11, of which waited for: 3 -> 6; matrix products, arithmetic and copies ran while one was open for 0% -> 0% of each run, Pallas kernels for 5% -> 4%
where the time goes in v6:
time: 59.8 us; the launch traced here: 59.5 us
  waiting for transfers between devices  21.3 us (36%)
  starting transfers between devices  15.5 us (26%)
  Pallas kernels  12 us (20%)
  local copies, waits for them, and re-layouts  10.6 us (18%)
    all_to_all x1, waiting for transfers between devices, per_device(): got = lax.all_to_all(partials, ('row', 'col'), 0, 0, tiled=True)  12 us
    unnamed x6, local copies, waits for them, and re-layouts  10.6 us
    ppermute x10, waiting for transfers between devices, exchange(): return lax.ppermute(x, axis, [(i, i ^ bit) for i in range(size)])  9.32 us
    ppermute x10, starting transfers between devices, exchange(): return lax.ppermute(x, axis, [(i, i ^ bit) for i in range(size)])  8.21 us
    pallas_call x1, Pallas kernels, partials_call(): pl.pallas_call(functools.partial(partials_kernel, n_col), in_specs=[pl.Bl...  7.6 us
    all_to_all x1, starting transfers between devices, per_device(): got = lax.all_to_all(partials, ('row', 'col'), 0, 0, tiled=True)  7.33 us
    pallas_call x3, Pallas kernels, product_call(): pl.pallas_call(functools.partial(product_kernel, at, first is not None),...  3.31 us
  transfers between devices with their start and end apart: 11, of which 6 were waited for; matrix products, arithmetic and copies ran while one was open for 0% of the time, Pallas kernels for 4%

profile of v6, /device:TPU:0, one launch (start us, length us, event | category | flops | bytes accessed | tf_op | source)
XLA Modules:
  0.0 59.5 jit_solution(9727642967071370591)
XLA Ops:
  0.0 7.6 %partials.1 = f32[32,5,4,128]{3,2,1,0:T(4,128)} custom-call(s32[1,32]{1,0:T(1,128)} %bitcast.4, bf16[256,4096]{1,0:T(8,128)(2,1)} %x_in.1, bf16[256,14336]{1,0:T(8,128)(2,1)} %x_out.1, bf16[4096,128]{1,0:T(8,128)(2,1)} %w_in.1, bf16[14336,128]{1,0:T(8,128)(2,1)} %w_out.1, f32[2048,4096]{1,0:T(8,128)} %refs_1_.3), custom_call_target="tpu_custom_call" | custom-call | tf_op jit(solution)/shard_map/partials/pallas_call | solution.py:78
  7.6 7.3 %all-to-all-start = ((f32[32,5,4,128]{3,2,1,0:T(4,128)}), f32[32,5,4,128]{3,2,1,0:T(4,128)S(1)}, u32[]{:S(2)}, u32[]{:S(2)}) async-start(f32[32,5,4,128]{3,2,1,0:T(4,128)} %partials.1), calls=%async_computation | async-start | bytes 655360 | tf_op jit(solution)/shard_map/all_to_all | solution.py:259
  15.0 12.0 %all-to-all-done = f32[32,5,4,128]{3,2,1,0:T(4,128)S(1)} async-done(((f32[32,5,4,128]{3,2,1,0:T(4,128)}), f32[32,5,4,128]{3,2,1,0:T(4,128)S(1)}, u32[]{:S(2)}, u32[]{:S(2)}) %all-to-all-start) | async-done | bytes 327712 | tf_op jit(solution)/shard_map/all_to_all | solution.py:259
  27.0 0.5 combine.1.refs_0_
  27.5 0.2 collective-permute-start
  27.7 0.3 collective-permute-start.2
  27.9 3.8 %collective-permute-done.refs_0_ = f32[32,512]{1,0:T(8,128)S(1)} collective-permute-done((f32[32,512]{1,0:T(8,128)S(1)}, f32[32,512]{1,0:T(8,128)S(1)}, u32[]{:S(2)}, u32[]{:S(2)}) %collective-permute-start) | collective-permute-done | bytes 65568 | tf_op jit(solution)/shard_map/ppermute | solution.py:243
  31.8 10.5 %copy-done = f32[2048,4096]{1,0:T(8,128)S(1)} copy-done((f32[2048,4096]{1,0:T(8,128)S(1)}, f32[2048,4096]{1,0:T(8,128)}, u32[]{:S(2)}) %copy-start) | copy-done | bytes 33554456
  42.3 1.6 %shard_map.73.refs_2_ = f32[32,4096]{1,0:T(8,128)S(1)} custom-call(f32[32,512]{1,0:T(8,128)S(1)} %combine.1.refs_0_, f32[32,512]{1,0:T(8,128)S(1)} %collective-permute-done.2.refs_1_, f32[2048,4096]{1,0:T(8,128)S(1)} %copy-done), custom_call_target="tpu_custom_call" | custom-call | tf_op jit(solution)/shard_map/pallas_call | solution.py:195
  43.9 0.9 %shard_map.74.refs_2_ = f32[32,4096]{1,0:T(8,128)S(1)} custom-call(f32[32,512]{1,0:T(8,128)S(1)} %collective-permute-done.refs_0_, f32[2048,4096]{1,0:T(8,128)S(1)} %copy-done, f32[32,4096]{1,0:T(8,128)S(1)} %shard_map.73.refs_2_), custom_call_target="tpu_custom_call" | custom-call | tf_op jit(solution)/shard_map/pallas_call | solution.py:195
  44.7 0.0 collective-permute-done.1.refs_0_
  44.7 0.9 %shard_map.75 = (f32[1,4,4096]{2,1,0:T(4,128)S(1)}, f32[1,4,4096]{2,1,0:T(4,128)S(1)}, f32[1,4,4096]{2,1,0:T(4,128)S(1)}, f32[1,4,4096]{2,1,0:T(4,128)S(1)}, f32...) custom-call(f32[32,512]{1,0:T(8,128)S(1)} %collective-permute-done.1.refs_0_, ...), custom_call_target="tpu_custom_call" | custom-call | tf_op jit(solution)/shard_map/pallas_call | solution.py:195
  45.6 0.8 %collective-permute-start.6 = (f32[1,4,4096]{2,1,0:T(4,128)S(1)}, f32[1,4,4096]{2,1,0:T(4,128)S(1)}, u32[]{:S(2)}, u32[]{:S(2)}) collective-permute-start(f32[1,4,4096]{2,1,0:T(4,128)S(1)} %get-tuple-element.18), channel_id=1, source_target_pairs={{0,4},{4,0},{8,12},{12,8},{16,20},{20,16},{24,28},{28,24},{1,5},{5... | collective-permute-start | bytes 196616 | tf_op jit(solution)/shard_map/ppermute | solution.py:243
  46.4 0.7 %collective-permute-start.7 = (f32[1,4,4096]{2,1,0:T(4,128)S(1)}, f32[1,4,4096]{2,1,0:T(4,128)S(1)}, u32[]{:S(2)}, u32[]{:S(2)}) collective-permute-start(f32[1,4,4096]{2,1,0:T(4,128)S(1)} %get-tuple-element.19), channel_id=1, source_target_pairs={{0,8},{4,12},{8,0},{12,4},{16,24},{20,28},{24,16},{28,20},{1,9},{5... | collective-permute-start | bytes 196616 | tf_op jit(solution)/shard_map/ppermute | solution.py:243
  47.1 2.1 %collective-permute-start.8 = (f32[1,4,4096]{2,1,0:T(4,128)S(1)}, f32[1,4,4096]{2,1,0:T(4,128)S(1)}, u32[]{:S(2)}, u32[]{:S(2)}) collective-permute-start(f32[1,4,4096]{2,1,0:T(4,128)S(1)} %get-tuple-element.20), channel_id=1, source_target_pairs={{0,12},{4,8},{8,4},{12,0},{16,28},{20,24},{24,20},{28,16},{1,13},{... | collective-permute-start | bytes 196616 | tf_op jit(solution)/shard_map/ppermute | solution.py:243
  49.2 0.8 %collective-permute-start.3 = (f32[4,4096]{1,0:T(4,128)S(1)}, f32[4,4096]{1,0:T(4,128)S(1)}, u32[]{:S(2)}, u32[]{:S(2)}) collective-permute-start(f32[4,4096]{1,0:T(4,128)S(1)} %get-tuple-element.14), channel_id=1, source_target_pairs={{0,4},{4,0},{8,12},{12,8},{16,20},{20,16},{24,28},{28,24},{1,5},{5... | collective-permute-start | bytes 196616 | tf_op jit(solution)/shard_map/ppermute | solution.py:243
  49.9 0.7 %collective-permute-start.4 = (f32[4,4096]{1,0:T(4,128)S(1)}, f32[4,4096]{1,0:T(4,128)S(1)}, u32[]{:S(2)}, u32[]{:S(2)}) collective-permute-start(f32[4,4096]{1,0:T(4,128)S(1)} %get-tuple-element.15), channel_id=1, source_target_pairs={{0,8},{4,12},{8,0},{12,4},{16,24},{20,28},{24,16},{28,20},{1,9},{5... | collective-permute-start | bytes 196616 | tf_op jit(solution)/shard_map/ppermute | solution.py:243
  50.6 2.1 %collective-permute-start.5 = (f32[4,4096]{1,0:T(4,128)S(1)}, f32[4,4096]{1,0:T(4,128)S(1)}, u32[]{:S(2)}, u32[]{:S(2)}) collective-permute-start(f32[4,4096]{1,0:T(4,128)S(1)} %get-tuple-element.16), channel_id=1, source_target_pairs={{0,12},{4,8},{8,4},{12,0},{16,28},{20,24},{24,20},{28,16},{1,13},{... | collective-permute-start | bytes 196616 | tf_op jit(solution)/shard_map/ppermute | solution.py:243
  52.7 0.3 collective-permute-done.8.refs_3_
  53.0 0.7 %collective-permute-start.9 = (f32[4,4096]{1,0:T(4,128)S(1)}, f32[4,4096]{1,0:T(4,128)S(1)}, u32[]{:S(2)}, u32[]{:S(2)}) collective-permute-start(f32[4,4096]{1,0:T(4,128)S(1)} %fold.1), channel_id=1, source_target_pairs={{0,16},{4,20},{8,24},{12,28},{16,0},{20,4},{24,8},{28,12},{1,17},{... | collective-permute-start | bytes 196616 | tf_op jit(solution)/shard_map/ppermute | solution.py:243
  53.7 0.9 %collective-permute-done.3.refs_1_ = f32[4,4096]{1,0:T(4,128)S(1)} collective-permute-done((f32[4,4096]{1,0:T(4,128)S(1)}, f32[4,4096]{1,0:T(4,128)S(1)}, u32[]{:S(2)}, u32[]{:S(2)}) %collective-permute-start.3) | collective-permute-done | bytes 65568 | tf_op jit(solution)/shard_map/ppermute | solution.py:243
  54.6 1.2 %collective-permute-done.5.refs_3_ = f32[4,4096]{1,0:T(4,128)S(1)} collective-permute-done((f32[4,4096]{1,0:T(4,128)S(1)}, f32[4,4096]{1,0:T(4,128)S(1)}, u32[]{:S(2)}, u32[]{:S(2)}) %collective-permute-start.5) | collective-permute-done | bytes 65568 | tf_op jit(solution)/shard_map/ppermute | solution.py:243
  55.8 3.1 %collective-permute-done.9.refs_4_ = f32[4,4096]{1,0:T(4,128)S(1)} collective-permute-done((f32[4,4096]{1,0:T(4,128)S(1)}, f32[4,4096]{1,0:T(4,128)S(1)}, u32[]{:S(2)}, u32[]{:S(2)}) %collective-permute-start.9) | collective-permute-done | bytes 65568 | tf_op jit(solution)/shard_map/ppermute | solution.py:243
  58.9 0.6 %finish.1 = f32[4,4096]{1,0:T(4,128)} custom-call(f32[4,4096]{1,0:T(4,128)S(1)} %get-tuple-element.13.refs_0_, f32[4,4096]{1,0:T(4,128)S(1)} %collective-permute-done.3.refs_1_, f32[4,4096]{1,0:T(4,128)S(1)} %collective-permute-done.4.refs_2_, f32[4,4096]{1,0:T(4,128)S(1)} %collective-permute-done.5.refs_3_, f32[4,4096]{1,0:T(4,128)S(1)} %collective-permute-done.9.refs_4_), custom_call_target="tpu_custom_call" | custom-call | tf_op jit(solution)/shard_map/finish/pallas_call | solution.py:231
  (13 shorter events, 0.0 us)
Async XLA Ops:
  7.6 19.4 %all-to-all-start = ((f32[32,5,4,128]{3,2,1,0:T(4,128)}), f32[32,5,4,128]{3,2,1,0:T(4,128)S(1)}, u32[]{:S(2)}, u32[]{:S(2)}) async-start(f32[32,5,4,128]{3,2,1,0:T(4,128)} %partials.1), calls=%async_computation | async-start | bytes 655360 | tf_op jit(solution)/shard_map/all_to_all | solution.py:259
  15.0 12.0 %copy-start.1 = (s32[32]{0:T(128)S(1)}, s32[32]{0:T(128)}, u32[]{:S(2)}) copy-start(s32[32]{0:T(128)} %param.11) | copy-start | bytes 388
  15.0 12.0 %copy-start.2 = (s32[32]{0:T(128)S(1)}, s32[32]{0:T(128)}, u32[]{:S(2)}) copy-start(s32[32]{0:T(128)} %param.12) | copy-start | bytes 388
  27.5 4.3 %collective-permute-start = (f32[32,512]{1,0:T(8,128)S(1)}, f32[32,512]{1,0:T(8,128)S(1)}, u32[]{:S(2)}, u32[]{:S(2)}) collective-permute-start(f32[32,512]{1,0:T(8,128)S(1)} %combine.1.refs_0_), channel_id=1, source_target_pairs={{0,2},{1,3},{2,0},{3,1},{4,6},{5,7},{6,4},{7,5},{8,10},{9,11},{10,... | collective-permute-start | bytes 196616 | tf_op jit(solution)/shard_map/ppermute | solution.py:243
  27.7 4.1 %collective-permute-start.2 = (f32[32,512]{1,0:T(8,128)S(1)}, f32[32,512]{1,0:T(8,128)S(1)}, u32[]{:S(2)}, u32[]{:S(2)}) collective-permute-start(f32[32,512]{1,0:T(8,128)S(1)} %combine.1.refs_0_), channel_id=1, source_target_pairs={{0,1},{1,0},{2,3},{3,2},{4,5},{5,4},{6,7},{7,6},{8,9},{9,8},{10,11... | collective-permute-start | bytes 196616 | tf_op jit(solution)/shard_map/ppermute | solution.py:243
  31.7 13.0 %collective-permute-start.1 = (f32[32,512]{1,0:T(8,128)S(1)}, f32[32,512]{1,0:T(8,128)S(1)}, u32[]{:S(2)}, u32[]{:S(2)}) collective-permute-start(f32[32,512]{1,0:T(8,128)S(1)} %collective-permute-done.refs_0_), channel_id=1, source_target_pairs={{0,1},{1,0},{2,3},{3,2},{4,5},{5,4},{6,7},{7,6},{8,9},{9,8},{10,11... | collective-permute-start | bytes 196616 | tf_op jit(solution)/shard_map/ppermute | solution.py:243
  31.7 10.5 %copy-start = (f32[2048,4096]{1,0:T(8,128)S(1)}, f32[2048,4096]{1,0:T(8,128)}, u32[]{:S(2)}) copy-start(f32[2048,4096]{1,0:T(8,128)} %refs_1_.3) | copy-start | bytes 100663296
  45.6 5.0 %collective-permute-start.6 = (f32[1,4,4096]{2,1,0:T(4,128)S(1)}, f32[1,4,4096]{2,1,0:T(4,128)S(1)}, u32[]{:S(2)}, u32[]{:S(2)}) collective-permute-start(f32[1,4,4096]{2,1,0:T(4,128)S(1)} %get-tuple-element.18), channel_id=1, source_target_pairs={{0,4},{4,0},{8,12},{12,8},{16,20},{20,16},{24,28},{28,24},{1,5},{5... | collective-permute-start | bytes 196616 | tf_op jit(solution)/shard_map/ppermute | solution.py:243
  46.4 6.2 %collective-permute-start.7 = (f32[1,4,4096]{2,1,0:T(4,128)S(1)}, f32[1,4,4096]{2,1,0:T(4,128)S(1)}, u32[]{:S(2)}, u32[]{:S(2)}) collective-permute-start(f32[1,4,4096]{2,1,0:T(4,128)S(1)} %get-tuple-element.19), channel_id=1, source_target_pairs={{0,8},{4,12},{8,0},{12,4},{16,24},{20,28},{24,16},{28,20},{1,9},{5... | collective-permute-start | bytes 196616 | tf_op jit(solution)/shard_map/ppermute | solution.py:243
  47.1 5.8 %collective-permute-start.8 = (f32[1,4,4096]{2,1,0:T(4,128)S(1)}, f32[1,4,4096]{2,1,0:T(4,128)S(1)}, u32[]{:S(2)}, u32[]{:S(2)}) collective-permute-start(f32[1,4,4096]{2,1,0:T(4,128)S(1)} %get-tuple-element.20), channel_id=1, source_target_pairs={{0,12},{4,8},{8,4},{12,0},{16,28},{20,24},{24,20},{28,16},{1,13},{... | collective-permute-start | bytes 196616 | tf_op jit(solution)/shard_map/ppermute | solution.py:243
  49.2 5.4 %collective-permute-start.3 = (f32[4,4096]{1,0:T(4,128)S(1)}, f32[4,4096]{1,0:T(4,128)S(1)}, u32[]{:S(2)}, u32[]{:S(2)}) collective-permute-start(f32[4,4096]{1,0:T(4,128)S(1)} %get-tuple-element.14), channel_id=1, source_target_pairs={{0,4},{4,0},{8,12},{12,8},{16,20},{20,16},{24,28},{28,24},{1,5},{5... | collective-permute-start | bytes 196616 | tf_op jit(solution)/shard_map/ppermute | solution.py:243
  49.9 4.6 %collective-permute-start.4 = (f32[4,4096]{1,0:T(4,128)S(1)}, f32[4,4096]{1,0:T(4,128)S(1)}, u32[]{:S(2)}, u32[]{:S(2)}) collective-permute-start(f32[4,4096]{1,0:T(4,128)S(1)} %get-tuple-element.15), channel_id=1, source_target_pairs={{0,8},{4,12},{8,0},{12,4},{16,24},{20,28},{24,16},{28,20},{1,9},{5... | collective-permute-start | bytes 196616 | tf_op jit(solution)/shard_map/ppermute | solution.py:243
  50.6 5.2 %collective-permute-start.5 = (f32[4,4096]{1,0:T(4,128)S(1)}, f32[4,4096]{1,0:T(4,128)S(1)}, u32[]{:S(2)}, u32[]{:S(2)}) collective-permute-start(f32[4,4096]{1,0:T(4,128)S(1)} %get-tuple-element.16), channel_id=1, source_target_pairs={{0,12},{4,8},{8,4},{12,0},{16,28},{20,24},{24,20},{28,16},{1,13},{... | collective-permute-start | bytes 196616 | tf_op jit(solution)/shard_map/ppermute | solution.py:243
  53.0 5.9 %collective-permute-start.9 = (f32[4,4096]{1,0:T(4,128)S(1)}, f32[4,4096]{1,0:T(4,128)S(1)}, u32[]{:S(2)}, u32[]{:S(2)}) collective-permute-start(f32[4,4096]{1,0:T(4,128)S(1)} %fold.1), channel_id=1, source_target_pairs={{0,16},{4,20},{8,24},{12,28},{16,0},{20,4},{24,8},{28,12},{1,17},{... | collective-permute-start | bytes 196616 | tf_op jit(solution)/shard_map/ppermute | solution.py:243
